TPU v7x, 32 devices: a whole 2x2x4 slice. The times are simulated.
32 devices in a mesh: space: 8 (over y, x, core), group: 4 (over z).
Axes of the slice: x: 2, y: 2, z: 4, core: 2. Of those that a mesh axis runs over, the one named last changes fastest.
Arguments:
- snapshot_basis: bfloat16 [65536, 1024], P('space', 'group'), may hold values from -40 to 40
- sketch: float32 [2, 512, 256], replicated, may hold values from -0.25 to 0.25
Outputs:
- merged_basis: bfloat16 [65536, 256], P(('space', 'group'))
All inputs are finite; a program needn't handle non-finite values.
Results may differ from a plain program's by a relative error of at most 0.0067.
Values may be sent and summed in bfloat16 or wider, within the bound.
No kernel may reach another device: no remote copies, remote signals or barrier semaphores. Data moves between devices by JAX's collectives and lax.ppermute only.
A program may use at most 128 MiB of HBM per device.

v0:
```python
import functools

import jax
import jax.numpy as jnp
from jax import lax
from jax.experimental import pallas as pl
from jax.experimental.pallas import tpu as pltpu
from jax.sharding import PartitionSpec as P


STEPS = 5
F32 = jnp.float32
BF16 = jnp.bfloat16
HBM = pl.BlockSpec(memory_space=pltpu.HBM)
SMEM = pl.BlockSpec(memory_space=pltpu.SMEM)
VMEM = pl.BlockSpec(memory_space=pltpu.VMEM)


def swap(block, axis, offset):
    count = lax.axis_size(axis)
    return lax.ppermute(block, axis, [(i, i ^ offset) for i in range(count)])


def send(value, routes):
    return lax.ppermute(value, "group", routes)


def after(value, *others):
    return lax.optimization_barrier((value,) + others)[0]


def dot_t(a, b):
    return lax.dot_general(a, b, (((0,), (0,)), ((), ())), preferred_element_type=F32)


def dot(a, b):
    return jnp.dot(a, b, preferred_element_type=F32)


def split(x):
    high = x.astype(BF16)
    return high, (x - high.astype(F32)).astype(BF16)


def dot3(a, b):
    ah, al = a
    bh, bl = b
    return dot(ah, bh) + (dot(ah, bl) + dot(al, bh))


def shape(dims, kind):
    return jax.ShapeDtypeStruct(dims, kind)


def call(kernel, mib, in_specs, outs, scratch, *args):
    return pl.pallas_call(
        kernel,
        in_specs=in_specs,
        out_specs=[VMEM] * len(outs),
        out_shape=outs,
        scratch_shapes=scratch,
        compiler_params=pltpu.CompilerParams(vmem_limit_bytes=mib * 2**20),
    )(*args)


def pick_kernel(cuts, x_ref, *refs):
    outs, sems = refs[:-1], refs[-1]
    groups = lax.axis_size("group")
    block_rows = x_ref.shape[0] // groups
    member = lax.axis_index("group")
    bit0 = member & 1
    bit1 = member >> 1 & 1
    copies = []
    for out, (flip1, flip0, begin) in zip(outs, cuts):
        for h in range(out.shape[0]):
            block = h * 4 + jnp.bitwise_xor(bit1, flip1) * 2 + jnp.bitwise_xor(bit0, flip0)
            start = pl.multiple_of(block * block_rows + begin, 256)
            copies.append(
                pltpu.make_async_copy(
                    x_ref.at[pl.ds(start, out.shape[1]), :], out.at[h], sems.at[len(copies)]
                )
            )
    for copy in copies:
        copy.start()
    for copy in copies:
        copy.wait()


def pick(panel, mib, cuts):
    _, width = panel.shape
    outer = lax.axis_size("group") // 4
    outs = [shape((outer, size, width), BF16) for _, _, _, size in cuts]
    sems = pltpu.SemaphoreType.DMA((len(cuts) * outer,))
    return call(
        functools.partial(pick_kernel, [cut[:3] for cut in cuts]),
        mib, [HBM], outs, [sems], panel,
    )


def place(me, offset, rows, width):
    device = jnp.bitwise_xor(me, offset)
    start = (device & 1) * (width // 2) + (device >> 1) * rows
    return pl.multiple_of(start, rows)


def write_halves(me, acc, mine, sent):
    rows = mine.shape[0]
    mine[...] = acc[pl.ds(pl.multiple_of((me & 1) * rows, rows), rows), :]
    sent[...] = acc[pl.ds(pl.multiple_of((1 - (me & 1)) * rows, rows), rows), :]


def halves(width):
    return [shape((width // 2, width), F32)] * 2


def divide_kernel(x, head, tail):
    head[...] = x[:, : head.shape[1], :]
    tail[...] = x[:, head.shape[1] :, :]


def divide(x, part):
    outer, rows, width = x.shape
    outs = [shape((outer, size, width), x.dtype) for size in (part, rows - part)]
    return call(divide_kernel, 4, [VMEM], outs, [], x)


def own_gram_kernel(ids, *refs):
    blocks, (mine, sent, acc) = refs[:-3], refs[-3:]
    total = None
    for block in blocks:
        for h in range(block.shape[0]):
            x = block[h]
            part = dot_t(x, x)
            total = part if total is None else total + part
    acc[...] = total
    write_halves(ids[0], acc, mine, sent)


def own_gram(ids, blocks):
    width = blocks[0].shape[-1]
    scratch = [pltpu.VMEM((width, width), F32)]
    return call(
        own_gram_kernel, 12, [SMEM] + [VMEM] * len(blocks), halves(width), scratch,
        ids, *blocks,
    )


def cross_kernel(begin, chained, last, ids, own, other, *refs):
    if chained:
        start, refs = refs[0], refs[1:]
    outs, acc = refs[:-1], refs[-1]
    rows = other.shape[1]

    def add(flip):
        total = start[...] if chained else None
        for h in range(other.shape[0]):
            pair = (own[h, begin : begin + rows, :], other[h])
            part = dot_t(pair[flip], pair[1 - flip])
            total = part if total is None else total + part
        acc[...] = total

    pl.when(ids[1] == 0)(lambda: add(0))
    pl.when(ids[1] == 1)(lambda: add(1))
    if last:
        write_halves(ids[0], acc, *outs)
    else:
        outs[0][...] = acc[...]


def cross_gram(ids, own, other, begin, start, last):
    width = own.shape[-1]
    chained = start is not None
    outs = halves(width) if last else [shape((width, width), F32)]
    return call(
        functools.partial(cross_kernel, begin, chained, last),
        8, [SMEM] + [VMEM] * (2 + chained), outs,
        [pltpu.VMEM((width, width), F32)],
        ids, own, other, *([start] if chained else []),
    )


def share_kernel(ids, mine, got, *refs):
    outs, acc = refs[:-1], refs[-1]
    acc[...] = mine[...] + got[...]
    rows = outs[0].shape[0]
    for k, out in enumerate(outs):
        start = pl.multiple_of(jnp.bitwise_xor(ids[0] >> 1, k) * rows, rows)
        out[...] = acc[pl.ds(start, rows), :]


def scatter_space(ids, mine, sent):
    chips = lax.axis_size("space") // 2
    rows, width = mine.shape
    got = swap(sent, "space", 1)
    slices = call(
        share_kernel, 4, [SMEM, VMEM, VMEM],
        [shape((rows // chips, width), F32)] * chips, [pltpu.VMEM((rows, width), F32)],
        ids, mine, got,
    )
    total = slices[0]
    got = [swap(slices[k], "space", 2 * k) for k in range(1, chips)]
    for piece in got:
        total = total + piece
    return total


def gather_space(piece):
    count = lax.axis_size("space")
    pieces = [piece] + [None] * (count - 1)
    for k in range(2, count, 2):
        pieces[k] = swap(piece, "space", k)
    for k in range(0, count, 2):
        pieces[k + 1] = swap(pieces[k], "space", 1)
    return pieces


def assemble_kernel(ids, *refs):
    pieces, out = refs[:-1], refs[-1]
    rows, width = pieces[0].shape[1:]
    for k, piece in enumerate(pieces):
        out[:, pl.ds(place(ids[0], k, rows, width), rows), :] = piece[...]


def assemble(ids, pieces):
    lead, rows, width = pieces[0].shape
    return call(
        assemble_kernel, 4, [SMEM] + [VMEM] * len(pieces),
        [shape((lead, rows * len(pieces), width), F32)], [], ids, *pieces,
    )[0]


def run_filter(pairs, ids, diag, given, pieces, gram, iterate):
    rows, width = pieces[0].shape[1:]
    full = 2 * width
    for p in range(pairs):
        gram[p, :width, :width] = diag[2 * p]
        gram[p, width:, width:] = diag[2 * p + 1]
        for k, piece in enumerate(pieces):
            gram[p, pl.ds(place(ids[0], k, rows, width), rows), width:] = piece[p]
        gram[p, width:, :width] = gram[p, :width, width:].T
    eye = lax.broadcasted_iota(jnp.int32, (full, full), 0) == lax.broadcasted_iota(
        jnp.int32, (full, full), 1
    )
    for p in range(pairs):
        whole = gram[p]
        trace = jnp.sum(jnp.where(eye, whole, 0.0), keepdims=True)
        shifted = whole / (trace / full) - jnp.where(eye, 1.0, 0.0)
        norm = jnp.sqrt(jnp.sum(shifted * shifted, keepdims=True))
        iterate[p] = shifted / (1.0 + norm)

    def step(_, carry):
        xs = [iterate[p] for p in range(pairs)]
        short = [x.astype(BF16) for x in xs]
        squares = [dot(x, x).astype(BF16) for x in short]
        for p in range(pairs):
            iterate[p] = 1.5 * xs[p] - 0.5 * dot(short[p], squares[p])
        return carry

    lax.fori_loop(0, STEPS - 1, step, 0)
    given_parts = split(given)
    parts = [split(iterate[p]) for p in range(pairs)]
    first = [dot3(part, given_parts) for part in parts]
    second = [dot3(part, split(t)) for part, t in zip(parts, first)]
    third = [dot3(part, split(t)) for part, t in zip(parts, second)]
    mixes = []
    for p in range(pairs):
        applied = 1.5 * first[p] - 0.5 * third[p]
        mixes.append((0.5 * (given + applied)).astype(BF16))
    return mixes


def pair_filter_kernel(ids, diag, sketch, *refs):
    pieces, (mix_ref, gram, iterate) = refs[:-3], refs[-3:]
    mixes = run_filter(2, ids, diag, sketch[0], pieces, gram, iterate)
    for p in range(2):
        mix_ref[p] = mixes[p].reshape(mix_ref.shape[1:])


def pair_filter(ids, diag, pieces, sketch):
    pairs, _, width = pieces[0].shape
    outs = [shape((pairs, 2, width, width), BF16), shape((pairs, 2 * width, 2 * width), F32)]
    return call(
        pair_filter_kernel, 20, [SMEM] + [VMEM] * (2 + len(pieces)), outs,
        [pltpu.VMEM((pairs, 2 * width, 2 * width), F32)],
        ids, diag, sketch, *pieces,
    )


def next_diag_kernel(gram, mix, out):
    for p in range(out.shape[0]):
        gh, gl = split(gram[p])
        m = mix[p].reshape(gh.shape[0], -1)
        th, tl = split(dot(gh, m) + dot(gl, m))
        out[p] = dot_t(m, th) + dot_t(m, tl)


def next_diag(gram, mix):
    pairs, _, width, _ = mix.shape
    return call(
        next_diag_kernel, 12, [VMEM] * 2, [shape((pairs, width, width), F32)], [],
        gram, mix,
    )[0]


def read(pieces, h, begin, size):
    for piece in pieces:
        if begin < piece.shape[1]:
            return piece[h, begin : begin + size, :]
        begin -= piece.shape[1]


def merge_own_kernel(ids, mix, mine, near_head, near_tail, out):
    bit0, bit1 = ids[1], ids[2]
    tile = min(512, near_head.shape[1], near_tail.shape[1])
    for h in range(mine.shape[0]):
        for b in range(0, mine.shape[1], tile):
            total = dot(mine[h, b : b + tile, :], mix[bit1, bit0])
            total += dot(read([near_head, near_tail], h, b, tile), mix[bit1, 1 - bit0])
            out[h, b : b + tile, :] = total.astype(BF16)


def merge_own(ids, mix, mine, *near):
    return call(
        merge_own_kernel, 8, [SMEM] + [VMEM] * 4, [shape(mine.shape, BF16)], [],
        ids, mix, mine, *near,
    )[0]


def merge_other_kernel(begin, chained, last, ids, mix, own, left, keep, passed, *refs):
    if chained:
        start, refs = refs[0], refs[1:]
    count = 3 if last else 2
    risen, (out, *outs, acc) = refs[: -count - 1], refs[-count - 1 :]
    bit0, bit1 = ids[1], ids[2]
    pair = 1 - bit1
    acc[...] = start[...] if chained else jnp.zeros(acc.shape, F32)
    outer, rows, _ = out.shape
    tile = min(256, rows)
    tile = 128 if rows % 256 else tile
    tiles = [(h, b) for h in range(outer) for b in range(0, rows, tile)]

    def merge(low, low_begin, high, high_begin):
        for h, b in tiles:
            total = dot(read(low, h, low_begin + b, tile), mix[pair, pair])
            total += dot(read(high, h, high_begin + b, tile), mix[pair, 1 - pair])
            out[h, b : b + tile, :] = total.astype(BF16)

    pl.when(bit0 != bit1)(lambda: merge([left], begin, [keep], begin))
    pl.when(bit0 == bit1)(lambda: merge(risen, begin, [passed], 0))

    def add(flip):
        for h in range(outer):
            both = (own[h, begin : begin + rows, :], out[h])
            acc[...] += dot_t(both[flip], both[1 - flip])

    pl.when(bit1 == 0)(lambda: add(0))
    pl.when(bit1 == 1)(lambda: add(1))
    if last:
        write_halves(ids[0], acc, *outs)
    else:
        outs[0][...] = acc[...]


def merge_other(ids, mix, own, begin, left, keep, passed, risen, start):
    width = own.shape[-1]
    chained = start is not None
    outs = halves(width) if chained else [shape((width, width), F32)]
    args = [ids, mix, own, left, keep, passed] + ([start] if chained else []) + risen
    return call(
        functools.partial(merge_other_kernel, begin, chained, chained), 12,
        [SMEM] + [VMEM] * (len(args) - 1), [shape(passed.shape, BF16)] + outs,
        [pltpu.VMEM((width, width), F32)], *args,
    )


def merge_filter_kernel(which, level, last, cuts, ids, diag, sketch, own, *refs):
    others, refs = refs[:cuts], refs[cuts:]
    count = 3 if last else 4
    pieces, refs = refs[:-count], refs[-count:]
    out, mix_ref, gram, iterate = refs[0], refs[-2 if last else 1], None, refs[-1]
    if last:
        gram = refs[-2]
        mix_ref = None
    else:
        gram = refs[2]
    mix = run_filter(1, ids, diag, sketch[level], pieces, gram, iterate)[0]
    width = diag.shape[-1]
    bit = ids[which]

    def finish(low, high):
        for h in range(own.shape[0]):
            for b in range(0, own.shape[1], tile):
                total = dot(read(low, h, b, tile), mix[:width])
                total += dot(read(high, h, b, tile), mix[width:])
                out[h, b : b + tile, :] = total.astype(BF16)

    tile = min(256, *(other.shape[1] & -other.shape[1] for other in others))
    pl.when(bit == 0)(lambda: finish([own], others))
    pl.when(bit == 1)(lambda: finish(others, [own]))
    if not last:
        mix_ref[0] = mix.reshape(mix_ref.shape[1:])


def merge_filter(ids, which, level, last, diag, pieces, sketch, own, others):
    width = diag.shape[-1]
    square = (1, 2 * width, 2 * width)
    outs = [shape(own.shape, BF16)]
    scratch = [pltpu.VMEM(square, F32)] * 2
    if not last:
        outs += [shape((1, 2, width, width), BF16), shape(square, F32)]
        scratch = scratch[:1]
    return call(
        functools.partial(merge_filter_kernel, which, level, last, len(others)),
        20, [SMEM] + [VMEM] * (3 + len(others) + len(pieces)), outs, scratch,
        ids, diag, sketch, own, *others, *pieces,
    )


def compute(snapshot_basis, sketch):
    rows, width = snapshot_basis.shape
    groups = lax.axis_size("group")
    levels = groups.bit_length() - 1
    member = lax.axis_index("group")
    bit0 = member & 1
    bit1 = member >> 1 & 1
    ids = jnp.stack([lax.axis_index("space"), bit0, bit1]).astype(jnp.int32)
    block_rows = rows // groups
    cut = block_rows * 3 // 4
    tail = block_rows - cut
    part = block_rows // 2

    middle, forward, rise, leave = [], [], [], []
    for base in range(0, groups, 4):
        middle += [(base + 1, base + 2), (base + 2, base + 1)]
        forward += [(base + 1, base), (base + 2, base + 3)]
        rise += [(base + 1, base + 3), (base + 2, base)]
        leave += [(base, base + 2), (base + 3, base + 1)]
    pair = [(i, i ^ 1) for i in range(groups)]

    far_own, across = pick(snapshot_basis, 59, [(1, 1, 0, block_rows), (1, 0, 0, block_rows)])
    far = send(far_own, pair)
    pass_on = send(across, middle)
    cuts = [(0, 1, 0, cut), (0, 1, cut, tail), (0, 0, 0, block_rows)]
    near_own, tail_own, mine = pick(after(snapshot_basis, far_own), 59, cuts)

    own_halves = own_gram(ids, [far_own, across, near_own, tail_own, mine])
    own_sum = scatter_space(ids, *own_halves)
    turned = [own_sum] + [swap(own_sum, "group", k) for k in (1, 2, 3)]

    near_head = send(after(near_own, own_sum), pair)
    keep = send(after(far_own, own_sum), middle)
    near_tail = send(after(tail_own, own_sum), pair)
    far_head, far_tail = divide(far, part)
    rise_head = send(after(far_head, own_sum), rise)

    quad = member & 3
    stacked = jnp.stack(turned)
    diag_slices = jnp.stack(
        [lax.dynamic_index_in_dim(stacked, quad ^ g, 0, keepdims=False) for g in range(4)]
    )
    diag = assemble(ids, gather_space(diag_slices))

    cross = cross_gram(ids, across, far, 0, None, False)[0]
    cross = cross_gram(ids, mine, near_head, 0, cross, False)[0]
    cross_halves = cross_gram(ids, mine, near_tail, cut, cross, True)
    cross_sum = scatter_space(ids, *cross_halves)
    here = cross_sum + send(cross_sum, pair)
    there = swap(here, "group", 2)
    both = jnp.stack([jnp.where(bit1 == 0, here, there), jnp.where(bit1 == 0, there, here)])

    pass_parts = divide(pass_on, cut)
    pass_head = send(after(pass_parts[0], here), forward)
    left = send(after(across, here), leave)
    rise_tail = send(after(far_tail, here), rise)
    pass_tail = send(after(pass_parts[1], here), forward)

    mix, gram = pair_filter(ids, diag, gather_space(both), sketch)
    diag = next_diag(gram, mix)
    own_merged = merge_own(ids, mix, mine, near_head, near_tail)
    other_head, cross = merge_other(
        ids, mix, own_merged, 0, left, keep, pass_head, [rise_head, rise_tail], None
    )
    other_tail, *both_halves = merge_other(
        ids, mix, own_merged, cut, left, keep, pass_tail, [rise_head, rise_tail],
        cross,
    )
    total = scatter_space(ids, *both_halves)
    one, two, three = [swap(total, "group", k) for k in (1, 2, 3)]
    total = (total + one) + (two + three)
    result = merge_filter(
        ids, 2, 1, levels == 2, diag, gather_space(total[None]), sketch,
        own_merged, [other_head, other_tail],
    )

    for level in range(2, levels):
        merged = result[0]
        bit = member >> level & 1
        pairs = merged.reshape(-1, 2, block_rows, width)
        kept = lax.dynamic_index_in_dim(pairs, bit, 1, keepdims=False)
        given = lax.dynamic_index_in_dim(pairs, 1 - bit, 1, keepdims=False)
        got = swap(given, "group", 1 << level)
        diag_own = next_diag(result[2], result[1])[0]
        diag_got = swap(diag_own, "group", 1 << level)
        flags = jnp.stack([lax.axis_index("space"), bit]).astype(jnp.int32)
        total = scatter_space(flags, *cross_gram(flags, kept, got, 0, None, True))
        for low in range(level + 1):
            total = total + swap(total, "group", 1 << low)
        diag = jnp.stack(
            [jnp.where(bit == 0, diag_own, diag_got), jnp.where(bit == 0, diag_got, diag_own)]
        )
        result = merge_filter(
            flags, 1, level, level + 1 == levels, diag, gather_space(total[None]),
            sketch, kept, [got],
        )
    return result[0].reshape(block_rows, width)


def solution(mesh):
    in_specs = (P("space", "group"), P())
    out_specs = P(("space", "group"), None)
    return jax.shard_map(compute, mesh=mesh, in_specs=in_specs, out_specs=out_specs, check_vma=False)
```

profile of v0, /device:TPU:0, one launch (start us, length us, event | category | flops | bytes accessed | tf_op | source)
XLA Modules:
  0.0 196.6 jit_solution(18002117902303335584)
XLA Ops:
  0.0 2.9 %shard_map.28 = (bf16[1,2048,256]{2,1,0:T(8,128)(2,1)}, bf16[1,2048,256]{2,1,0:T(8,128)(2,1)}) custom-call(bf16[8192,256]{1,0:T(8,128)(2,1)} %x_ref.2), custom_call_target="tpu_custom_call" | custom-call | tf_op jit(solution)/shard_map/pallas_call | solution.py:56
  2.9 3.0 %shard_map.29 = (bf16[1,1536,256]{2,1,0:T(8,128)(2,1)}, bf16[1,512,256]{2,1,0:T(8,128)(2,1)}, bf16[1,2048,256]{2,1,0:T(8,128)(2,1)}) custom-call(bf16[8192,256]{1,0:T(8,128)(2,1)} %x_ref.2), custom_call_target="tpu_custom_call" | custom-call | tf_op jit(solution)/shard_map/pallas_call | solution.py:56
  8.4 2.7 %shard_map.30 = (f32[128,256]{1,0:T(8,128)S(1)}, f32[128,256]{1,0:T(8,128)S(1)}) custom-call(s32[3]{0:T(128)S(1)} %pad_add_fusion.ids, bf16[1,2048,256]{2,1,0:T(8,128)(2,1)} %get-tuple-element.69.refs_0_, bf16[1,2048,256]{2,1,0:T(8,128)(2,1)S(1)} %copy-done.2, bf16[1,1536,256]{2,1,0:T(8,128)(2,1)S(1)} %copy-done.9, ...), custom_call_target="tpu_custom_call" | custom-call | tf_op jit(solution)/shard_map/pallas_call | solution.py:56
  11.6 2.6 %collective-permute-start.16 = (bf16[1,2048,256]{2,1,0:T(8,128)(2,1)}, bf16[1,2048,256]{2,1,0:T(8,128)(2,1)S(1)}, u32[]{:S(2)}, u32[]{:S(2)}) collective-permute-start(bf16[1,2048,256]{2,1,0:T(8,128)(2,1)} %get-tuple-element.69.refs_0_), channel_id=1, source_target_pairs={{0,1},{1,0},{2,3},{3,2},{4,5},{5,4},{6,7},{7,6},{8,9},{9,8},{10,11... | collective-permute-start | bytes 3145736 | tf_op jit(solution)/shard_map/ppermute | solution.py:25
  14.8 2.5 %collective-permute-start.3 = (f32[32,256]{1,0:T(8,128)S(1)}, f32[32,256]{1,0:T(8,128)S(1)}, u32[]{:S(2)}, u32[]{:S(2)}) collective-permute-start(f32[32,256]{1,0:T(8,128)S(1)} %get-tuple-element.57), channel_id=1, source_target_pairs={{0,24},{4,28},{8,16},{12,20},{16,8},{20,12},{24,0},{28,4},{1,25},{... | collective-permute-start | bytes 98312 | tf_op jit(solution)/shard_map/ppermute | solution.py:21
  23.1 1.6 collective-permute-start.32
  24.8 3.5 %collective-permute-start.14 = (bf16[1,512,256]{2,1,0:T(8,128)(2,1)}, bf16[1,512,256]{2,1,0:T(8,128)(2,1)S(1)}, u32[]{:S(2)}, u32[]{:S(2)}) collective-permute-start(bf16[1,512,256]{2,1,0:T(8,128)(2,1)} %get-tuple-element.58.refs_3_), channel_id=1, source_target_pairs={{0,1},{1,0},{2,3},{3,2},{4,5},{5,4},{6,7},{7,6},{8,9},{9,8},{10,11... | collective-permute-start | bytes 786440 | tf_op jit(solution)/shard_map/ppermute | solution.py:25
  29.1 26.2 %collective-permute-done.15.other.near_head = bf16[1,1536,256]{2,1,0:T(8,128)(2,1)S(1)} collective-permute-done((bf16[1,1536,256]{2,1,0:T(8,128)(2,1)S(1)}, bf16[1,1536,256]{2,1,0:T(8,128)(2,1)S(1)}, u32[]{:S(2)}, u32[]{:S(2)}) %collective-permute-start.15) | collective-permute-done | bytes 786464 | tf_op jit(solution)/shard_map/ppermute | solution.py:25
  56.3 3.0 %collective-permute-start.5 = (f32[32,256]{1,0:T(8,128)S(1)}, f32[32,256]{1,0:T(8,128)S(1)}, u32[]{:S(2)}, u32[]{:S(2)}) collective-permute-start(f32[32,256]{1,0:T(8,128)S(1)} %add_add_fusion.2), channel_id=1, source_target_pairs={{0,2},{1,3},{2,0},{3,1},{4,6},{5,7},{6,4},{7,5},{8,10},{9,11},{10,... | collective-permute-start | bytes 98312 | tf_op jit(solution)/shard_map/ppermute | solution.py:21
  64.1 1.8 collective-permute-start.31
  68.7 2.5 %collective-permute-start.20 = (f32[32,256]{1,0:T(8,128)S(1)}, f32[32,256]{1,0:T(8,128)S(1)}, u32[]{:S(2)}, u32[]{:S(2)}) collective-permute-start(f32[32,256]{1,0:T(8,128)S(1)} %get-tuple-element.65), channel_id=1, source_target_pairs={{0,24},{4,28},{8,16},{12,20},{16,8},{20,12},{24,0},{28,4},{1,25},{... | collective-permute-start | bytes 98312 | tf_op jit(solution)/shard_map/ppermute | solution.py:21
  80.2 1.9 collective-permute-start.12
  82.7 5.0 %collective-permute-start.30 = (bf16[1,2048,256]{2,1,0:T(8,128)(2,1)S(1)}, bf16[1,2048,256]{2,1,0:T(8,128)(2,1)}, u32[]{:S(2)}, u32[]{:S(2)}) collective-permute-start(bf16[1,2048,256]{2,1,0:T(8,128)(2,1)S(1)} %copy-done.2), channel_id=1, source_target_pairs={{0,2},{3,1},{4,6},{7,5},{8,10},{11,9},{12,14},{15,13},{16,18},{19,... | collective-permute-start | bytes 3145736 | tf_op jit(solution)/shard_map/ppermute | solution.py:25
  89.8 24.0 %collective-permute-done.22 = f32[32,256]{1,0:T(8,128)} collective-permute-done((f32[32,256]{1,0:T(8,128)}, f32[32,256]{1,0:T(8,128)}, u32[]{:S(2)}, u32[]{:S(2)}) %collective-permute-start.22) | collective-permute-done | bytes 32800 | tf_op jit(solution)/shard_map/ppermute | solution.py:21
  124.1 2.7 %collective-permute-done.28.refs_6_ = f32[2,32,256]{2,1,0:T(8,128)S(1)} collective-permute-done((f32[2,32,256]{2,1,0:T(8,128)S(1)}, f32[2,32,256]{2,1,0:T(8,128)S(1)}, u32[]{:S(2)}, u32[]{:S(2)}) %collective-permute-start.28) | collective-permute-done | bytes 65568 | tf_op jit(solution)/shard_map/ppermute | solution.py:21
  134.8 9.8 %shard_map.37 = (bf16[2,2,256,256]{3,2,1,0:T(8,128)(2,1)S(1)}, f32[2,512,512]{2,1,0:T(8,128)S(1)}) custom-call(s32[3]{0:T(128)S(1)} %pad_add_fusion.ids, f32[4,256,256]{2,1,0:T(8,128)S(1)} %shard_map.32.diag, f32[2,512,256]{2,1,0:T(8,128)S(1)} %copy-done.3, f32[2,32,256]{2,1,0:T(8,128)S(1)} %pad_maximum_fusion.2.refs_0_, ...), custom_call_target="tpu_custom_call" | custom-call | tf_op jit(solution)/shard_map/pallas_call | solution.py:56
  145.9 2.2 %collective-permute-done.35.refs_1_.refs_2_ = bf16[1,1024,256]{2,1,0:T(8,128)(2,1)S(1)} collective-permute-done((bf16[1,1024,256]{2,1,0:T(8,128)(2,1)S(1)}, bf16[1,1024,256]{2,1,0:T(8,128)(2,1)S(1)}, u32[]{:S(2)}, u32[]{:S(2)}) %collective-permute-start.35) | collective-permute-done | bytes 524320 | tf_op jit(solution)/shard_map/ppermute | solution.py:25
  148.1 10.4 %collective-permute-done.33.passed = bf16[1,1536,256]{2,1,0:T(8,128)(2,1)S(1)} collective-permute-done((bf16[1,1536,256]{2,1,0:T(8,128)(2,1)S(1)}, bf16[1,1536,256]{2,1,0:T(8,128)(2,1)S(1)}, u32[]{:S(2)}, u32[]{:S(2)}) %collective-permute-start.33) | collective-permute-done | bytes 786464 | tf_op jit(solution)/shard_map/ppermute | solution.py:25
  158.5 2.8 %shard_map.42 = (bf16[1,1536,256]{2,1,0:T(8,128)(2,1)S(1)}, f32[256,256]{1,0:T(8,128)S(1)}) custom-call(s32[3]{0:T(128)S(1)} %pad_add_fusion.ids, bf16[2,2,256,256]{3,2,1,0:T(8,128)(2,1)S(1)} %get-tuple-element.67.mix, bf16[1,2048,256]{2,1,0:T(8,128)(2,1)S(1)} %shard_map.39.own, bf16[1,2048,256]{2,1,0:T(8,128)(2,1)} %collective-permute-done.30.left, ...), custom_call_target="tpu_custom_call" | custom-call | tf_op jit(solution)/shard_map/pallas_call | solution.py:56
  162.5 2.2 %shard_map.43 = (bf16[1,512,256]{2,1,0:T(8,128)(2,1)S(1)}, f32[128,256]{1,0:T(8,128)S(1)}, f32[128,256]{1,0:T(8,128)S(1)}) custom-call(s32[3]{0:T(128)S(1)} %pad_add_fusion.ids, bf16[2,2,256,256]{3,2,1,0:T(8,128)(2,1)S(1)} %get-tuple-element.67.mix, bf16[1,2048,256]{2,1,0:T(8,128)(2,1)S(1)} %shard_map.39.own, ...), custom_call_target="tpu_custom_call" | custom-call | tf_op jit(solution)/shard_map/pallas_call | solution.py:56
  173.3 2.0 %collective-permute-start.43 = (f32[32,256]{1,0:T(8,128)S(1)}, f32[32,256]{1,0:T(8,128)S(1)}, u32[]{:S(2)}, u32[]{:S(2)}) collective-permute-start(f32[32,256]{1,0:T(8,128)S(1)} %add_add_fusion), channel_id=1, source_target_pairs={{0,3},{1,2},{2,1},{3,0},{4,7},{5,6},{6,5},{7,4},{8,11},{9,10},{10,... | collective-permute-start | bytes 98312 | tf_op jit(solution)/shard_map/ppermute | solution.py:21
  179.4 1.7 collective-permute-start.45
  186.2 1.9 shard_map.38.diag
  188.2 8.4 %shard_map.45 = bf16[1,2048,256]{2,1,0:T(8,128)(2,1)} custom-call(s32[3]{0:T(128)S(1)} %pad_add_fusion.ids, f32[2,256,256]{2,1,0:T(8,128)S(1)} %shard_map.38.diag, f32[2,512,256]{2,1,0:T(8,128)S(1)} %copy-done.3, bf16[1,2048,256]{2,1,0:T(8,128)(2,1)S(1)} %shard_map.39.own, bf16[1,1536,256]{2,1,0:T(8,128)(2,1)S(1)} %get-tuple-element.76.refs_0_, ...), custom_call_target="tpu_custom_call" | custom-call | tf_op jit(solution)/shard_map/pallas_call | solution.py:56
  (135 shorter events, 68.9 us)
Async XLA Ops:
  11.6 47.7 %collective-permute-start.16 = (bf16[1,2048,256]{2,1,0:T(8,128)(2,1)}, bf16[1,2048,256]{2,1,0:T(8,128)(2,1)S(1)}, u32[]{:S(2)}, u32[]{:S(2)}) collective-permute-start(bf16[1,2048,256]{2,1,0:T(8,128)(2,1)} %get-tuple-element.69.refs_0_), channel_id=1, source_target_pairs={{0,1},{1,0},{2,3},{3,2},{4,5},{5,4},{6,7},{7,6},{8,9},{9,8},{10,11... | collective-permute-start | bytes 3145736 | tf_op jit(solution)/shard_map/ppermute | solution.py:25
  21.8 33.5 %collective-permute-start.15 = (bf16[1,1536,256]{2,1,0:T(8,128)(2,1)S(1)}, bf16[1,1536,256]{2,1,0:T(8,128)(2,1)S(1)}, u32[]{:S(2)}, u32[]{:S(2)}) collective-permute-start(bf16[1,1536,256]{2,1,0:T(8,128)(2,1)S(1)} %copy-done.9), channel_id=1, source_target_pairs={{0,1},{1,0},{2,3},{3,2},{4,5},{5,4},{6,7},{7,6},{8,9},{9,8},{10,11... | collective-permute-start | bytes 2359304 | tf_op jit(solution)/shard_map/ppermute | solution.py:25
  23.1 64.7 %collective-permute-start.32 = (bf16[1,2048,256]{2,1,0:T(8,128)(2,1)S(1)}, bf16[1,2048,256]{2,1,0:T(8,128)(2,1)}, u32[]{:S(2)}, u32[]{:S(2)}) collective-permute-start(bf16[1,2048,256]{2,1,0:T(8,128)(2,1)S(1)} %copy-done.2), channel_id=1, source_target_pairs={{1,2},{2,1},{5,6},{6,5},{9,10},{10,9},{13,14},{14,13},{17,18},{18,... | collective-permute-start | bytes 3145736 | tf_op jit(solution)/shard_map/ppermute | solution.py:25
  24.8 39.3 %collective-permute-start.14 = (bf16[1,512,256]{2,1,0:T(8,128)(2,1)}, bf16[1,512,256]{2,1,0:T(8,128)(2,1)S(1)}, u32[]{:S(2)}, u32[]{:S(2)}) collective-permute-start(bf16[1,512,256]{2,1,0:T(8,128)(2,1)} %get-tuple-element.58.refs_3_), channel_id=1, source_target_pairs={{0,1},{1,0},{2,3},{3,2},{4,5},{5,4},{6,7},{7,6},{8,9},{9,8},{10,11... | collective-permute-start | bytes 786440 | tf_op jit(solution)/shard_map/ppermute | solution.py:25
  28.2 38.5 %collective-permute-start.6 = (f32[32,256]{1,0:T(8,128)S(1)}, f32[32,256]{1,0:T(8,128)S(1)}, u32[]{:S(2)}, u32[]{:S(2)}) collective-permute-start(f32[32,256]{1,0:T(8,128)S(1)} %add_add_fusion.2), channel_id=1, source_target_pairs={{0,3},{1,2},{2,1},{3,0},{4,7},{5,6},{6,5},{7,4},{8,11},{9,10},{10,... | collective-permute-start | bytes 98312 | tf_op jit(solution)/shard_map/ppermute | solution.py:21
  56.3 10.6 %collective-permute-start.5 = (f32[32,256]{1,0:T(8,128)S(1)}, f32[32,256]{1,0:T(8,128)S(1)}, u32[]{:S(2)}, u32[]{:S(2)}) collective-permute-start(f32[32,256]{1,0:T(8,128)S(1)} %add_add_fusion.2), channel_id=1, source_target_pairs={{0,2},{1,3},{2,0},{3,1},{4,6},{5,7},{6,4},{7,5},{8,10},{9,11},{10,... | collective-permute-start | bytes 98312 | tf_op jit(solution)/shard_map/ppermute | solution.py:21
  59.3 7.6 %collective-permute-start.4 = (f32[32,256]{1,0:T(8,128)S(1)}, f32[32,256]{1,0:T(8,128)S(1)}, u32[]{:S(2)}, u32[]{:S(2)}) collective-permute-start(f32[32,256]{1,0:T(8,128)S(1)} %add_add_fusion.2), channel_id=1, source_target_pairs={{0,1},{1,0},{2,3},{3,2},{4,5},{5,4},{6,7},{7,6},{8,9},{9,8},{10,11... | collective-permute-start | bytes 98312 | tf_op jit(solution)/shard_map/ppermute | solution.py:21
  64.1 53.4 %collective-permute-start.31 = (bf16[1,2048,256]{2,1,0:T(8,128)(2,1)}, bf16[1,2048,256]{2,1,0:T(8,128)(2,1)}, u32[]{:S(2)}, u32[]{:S(2)}) collective-permute-start(bf16[1,2048,256]{2,1,0:T(8,128)(2,1)} %get-tuple-element.69.refs_0_), channel_id=1, source_target_pairs={{1,2},{2,1},{5,6},{6,5},{9,10},{10,9},{13,14},{14,13},{17,18},{18,... | collective-permute-start | bytes 3145736 | tf_op jit(solution)/shard_map/ppermute | solution.py:25
  75.7 7.0 %collective-permute-start.10 = (f32[4,32,256]{2,1,0:T(8,128)S(1)}, f32[4,32,256]{2,1,0:T(8,128)S(1)}, u32[]{:S(2)}, u32[]{:S(2)}) collective-permute-start(f32[4,32,256]{2,1,0:T(8,128)S(1)} %pad_maximum_fusion.1.refs_0_), channel_id=1, source_target_pairs={{0,16},{4,20},{8,24},{12,28},{16,0},{20,4},{24,8},{28,12},{1,17},{... | collective-permute-start | bytes 393224 | tf_op jit(solution)/shard_map/ppermute | solution.py:21
  80.2 8.9 %collective-permute-start.12 = (f32[4,32,256]{2,1,0:T(8,128)S(1)}, f32[4,32,256]{2,1,0:T(8,128)}, u32[]{:S(2)}, u32[]{:S(2)}) collective-permute-start(f32[4,32,256]{2,1,0:T(8,128)S(1)} %pad_maximum_fusion.1.refs_0_), channel_id=1, source_target_pairs={{0,24},{4,28},{8,16},{12,20},{16,8},{20,12},{24,0},{28,4},{1,25},{... | collective-permute-start | bytes 393224 | tf_op jit(solution)/shard_map/ppermute | solution.py:21
  82.1 7.4 %collective-permute-start.9 = (f32[4,32,256]{2,1,0:T(8,128)}, f32[4,32,256]{2,1,0:T(8,128)}, u32[]{:S(2)}, u32[]{:S(2)}) collective-permute-start(f32[4,32,256]{2,1,0:T(8,128)} %collective-permute-done.8.refs_2_), channel_id=1, source_target_pairs={{0,4},{4,0},{8,12},{12,8},{16,20},{20,16},{24,28},{28,24},{1,5},{5... | collective-permute-start | bytes 393224 | tf_op jit(solution)/shard_map/ppermute | solution.py:21
  82.7 75.8 %collective-permute-start.30 = (bf16[1,2048,256]{2,1,0:T(8,128)(2,1)S(1)}, bf16[1,2048,256]{2,1,0:T(8,128)(2,1)}, u32[]{:S(2)}, u32[]{:S(2)}) collective-permute-start(bf16[1,2048,256]{2,1,0:T(8,128)(2,1)S(1)} %copy-done.2), channel_id=1, source_target_pairs={{0,2},{3,1},{4,6},{7,5},{8,10},{11,9},{12,14},{15,13},{16,18},{19,... | collective-permute-start | bytes 3145736 | tf_op jit(solution)/shard_map/ppermute | solution.py:25
  87.8 26.0 %collective-permute-start.22 = (f32[32,256]{1,0:T(8,128)}, f32[32,256]{1,0:T(8,128)}, u32[]{:S(2)}, u32[]{:S(2)}) collective-permute-start(f32[32,256]{1,0:T(8,128)} %add.62), channel_id=1, source_target_pairs={{0,2},{1,3},{2,0},{3,1},{4,6},{5,7},{6,4},{7,5},{8,10},{9,11},{10,... | collective-permute-start | bytes 98312 | tf_op jit(solution)/shard_map/ppermute | solution.py:21
  89.2 26.6 %collective-permute-start.11 = (f32[4,32,256]{2,1,0:T(8,128)}, f32[4,32,256]{2,1,0:T(8,128)S(1)}, u32[]{:S(2)}, u32[]{:S(2)}) collective-permute-start(f32[4,32,256]{2,1,0:T(8,128)} %copy-done.12), channel_id=1, source_target_pairs={{0,4},{4,0},{8,12},{12,8},{16,20},{20,16},{24,28},{28,24},{1,5},{5... | collective-permute-start | bytes 393224 | tf_op jit(solution)/shard_map/ppermute | solution.py:21
  89.5 26.4 %collective-permute-start.13 = (f32[4,32,256]{2,1,0:T(8,128)}, f32[4,32,256]{2,1,0:T(8,128)S(1)}, u32[]{:S(2)}, u32[]{:S(2)}) collective-permute-start(f32[4,32,256]{2,1,0:T(8,128)} %collective-permute-done.12.refs_6_), channel_id=1, source_target_pairs={{0,4},{4,0},{8,12},{12,8},{16,20},{20,16},{24,28},{28,24},{1,5},{5... | collective-permute-start | bytes 393224 | tf_op jit(solution)/shard_map/ppermute | solution.py:21
  113.7 44.8 %collective-permute-start.33 = (bf16[1,1536,256]{2,1,0:T(8,128)(2,1)S(1)}, bf16[1,1536,256]{2,1,0:T(8,128)(2,1)S(1)}, u32[]{:S(2)}, u32[]{:S(2)}) collective-permute-start(bf16[1,1536,256]{2,1,0:T(8,128)(2,1)S(1)} %get-tuple-element.71), channel_id=1, source_target_pairs={{1,0},{2,3},{5,4},{6,7},{9,8},{10,11},{13,12},{14,15},{17,16},{18,... | collective-permute-start | bytes 2359304 | tf_op jit(solution)/shard_map/ppermute | solution.py:25
  115.9 5.7 %collective-permute-start.24 = (f32[2,32,256]{2,1,0:T(8,128)S(1)}, f32[2,32,256]{2,1,0:T(8,128)S(1)}, u32[]{:S(2)}, u32[]{:S(2)}) collective-permute-start(f32[2,32,256]{2,1,0:T(8,128)S(1)} %pad_maximum_fusion.2.refs_0_), channel_id=1, source_target_pairs={{0,8},{4,12},{8,0},{12,4},{16,24},{20,28},{24,16},{28,20},{1,9},{5... | collective-permute-start | bytes 196616 | tf_op jit(solution)/shard_map/ppermute | solution.py:21
  117.5 5.4 %collective-permute-start.26 = (f32[2,32,256]{2,1,0:T(8,128)S(1)}, f32[2,32,256]{2,1,0:T(8,128)S(1)}, u32[]{:S(2)}, u32[]{:S(2)}) collective-permute-start(f32[2,32,256]{2,1,0:T(8,128)S(1)} %pad_maximum_fusion.2.refs_0_), channel_id=1, source_target_pairs={{0,16},{4,20},{8,24},{12,28},{16,0},{20,4},{24,8},{28,12},{1,17},{... | collective-permute-start | bytes 196616 | tf_op jit(solution)/shard_map/ppermute | solution.py:21
  120.3 25.6 %collective-permute-start.34 = (bf16[1,1024,256]{2,1,0:T(8,128)(2,1)S(1)}, bf16[1,1024,256]{2,1,0:T(8,128)(2,1)S(1)}, u32[]{:S(2)}, u32[]{:S(2)}) collective-permute-start(bf16[1,1024,256]{2,1,0:T(8,128)(2,1)S(1)} %get-tuple-element.73), channel_id=1, source_target_pairs={{1,3},{2,0},{5,7},{6,4},{9,11},{10,8},{13,15},{14,12},{17,19},{18,... | collective-permute-start | bytes 1572872 | tf_op jit(solution)/shard_map/ppermute | solution.py:25
  121.6 5.2 %collective-permute-start.28 = (f32[2,32,256]{2,1,0:T(8,128)S(1)}, f32[2,32,256]{2,1,0:T(8,128)S(1)}, u32[]{:S(2)}, u32[]{:S(2)}) collective-permute-start(f32[2,32,256]{2,1,0:T(8,128)S(1)} %pad_maximum_fusion.2.refs_0_), channel_id=1, source_target_pairs={{0,24},{4,28},{8,16},{12,20},{16,8},{20,12},{24,0},{28,4},{1,25},{... | collective-permute-start | bytes 196616 | tf_op jit(solution)/shard_map/ppermute | solution.py:21
  122.9 25.3 %collective-permute-start.35 = (bf16[1,1024,256]{2,1,0:T(8,128)(2,1)S(1)}, bf16[1,1024,256]{2,1,0:T(8,128)(2,1)S(1)}, u32[]{:S(2)}, u32[]{:S(2)}) collective-permute-start(bf16[1,1024,256]{2,1,0:T(8,128)(2,1)S(1)} %get-tuple-element.75), channel_id=1, source_target_pairs={{1,3},{2,0},{5,7},{6,4},{9,11},{10,8},{13,15},{14,12},{17,19},{18,... | collective-permute-start | bytes 1572872 | tf_op jit(solution)/shard_map/ppermute | solution.py:25
  130.6 31.9 %collective-permute-start.36 = (bf16[1,512,256]{2,1,0:T(8,128)(2,1)S(1)}, bf16[1,512,256]{2,1,0:T(8,128)(2,1)S(1)}, u32[]{:S(2)}, u32[]{:S(2)}) collective-permute-start(bf16[1,512,256]{2,1,0:T(8,128)(2,1)S(1)} %get-tuple-element.78), channel_id=1, source_target_pairs={{1,0},{2,3},{5,4},{6,7},{9,8},{10,11},{13,12},{14,15},{17,16},{18,... | collective-permute-start | bytes 786440 | tf_op jit(solution)/shard_map/ppermute | solution.py:25
  173.3 5.7 %collective-permute-start.43 = (f32[32,256]{1,0:T(8,128)S(1)}, f32[32,256]{1,0:T(8,128)S(1)}, u32[]{:S(2)}, u32[]{:S(2)}) collective-permute-start(f32[32,256]{1,0:T(8,128)S(1)} %add_add_fusion), channel_id=1, source_target_pairs={{0,3},{1,2},{2,1},{3,0},{4,7},{5,6},{6,5},{7,4},{8,11},{9,10},{10,... | collective-permute-start | bytes 98312 | tf_op jit(solution)/shard_map/ppermute | solution.py:21
  182.9 5.2 %collective-permute-start.44 = (f32[1,32,256]{2,1,0:T(8,128)S(1)}, f32[1,32,256]{2,1,0:T(8,128)S(1)}, u32[]{:S(2)}, u32[]{:S(2)}) collective-permute-start(f32[1,32,256]{2,1,0:T(8,128)S(1)} %add_bitcast_fusion.refs_2_), channel_id=1, source_target_pairs={{0,4},{4,0},{8,12},{12,8},{16,20},{20,16},{24,28},{28,24},{1,5},{5... | collective-permute-start | bytes 98312 | tf_op jit(solution)/shard_map/ppermute | solution.py:21
  (41 other events, 297.1 us)
where the time goes:
time: 197 us
  waiting for transfers between devices  89 us (45%)
  starting transfers between devices  55.5 us (28%)
  Pallas kernels  42 us (21%)
  local copies, waits for them, and re-layouts  8.13 us (4%)
    ppermute x40, waiting for transfers between devices, swap(): return lax.ppermute(block, axis, [(i, i ^ offset) for i in range(count)])  49 us
    pallas_call x18, Pallas kernels, call(): pl.pallas_call(kernel, in_specs=in_specs, out_specs=[VMEM] * len(outs), o...  42 us
    ppermute x11, waiting for transfers between devices, send(): return lax.ppermute(value, 'group', routes)  40 us
    ppermute x40, starting transfers between devices, swap(): return lax.ppermute(block, axis, [(i, i ^ offset) for i in range(count)])  33.2 us
    ppermute x11, starting transfers between devices, send(): return lax.ppermute(value, 'group', routes)  22.2 us
    unnamed x28, local copies, waits for them, and re-layouts  8.11 us
  transfers between devices with their start and end apart: 51, of which 26 were waited for; matrix products, arithmetic and copies ran while one was open for 1% of the time, Pallas kernels for 11%

commit v1 on v0

--- a/solution.py
+++ b/solution.py
@@ -1,4 +1,5 @@
 import functools
+import math
 
 import jax
 import jax.numpy as jnp
@@ -311,7 +312,7 @@
 
 def merge_own_kernel(ids, mix, mine, near_head, near_tail, out):
     bit0, bit1 = ids[1], ids[2]
-    tile = min(512, near_head.shape[1], near_tail.shape[1])
+    tile = math.gcd(512, near_head.shape[1], near_tail.shape[1])
     for h in range(mine.shape[0]):
         for b in range(0, mine.shape[1], tile):
             total = dot(mine[h, b : b + tile, :], mix[bit1, bit0])
@@ -326,49 +327,63 @@
     )[0]
 
 
-def merge_other_kernel(begin, chained, last, ids, mix, own, left, keep, passed, *refs):
+def merge_other_kernel(begin, segments, chained, ids, mix, own, keep, risen, *refs):
+    count = len(segments)
+    left, passed, refs = refs[:count], refs[count : 2 * count], refs[2 * count :]
     if chained:
         start, refs = refs[0], refs[1:]
-    count = 3 if last else 2
-    risen, (out, *outs, acc) = refs[: -count - 1], refs[-count - 1 :]
+    out, *outs, acc = refs
     bit0, bit1 = ids[1], ids[2]
     pair = 1 - bit1
     acc[...] = start[...] if chained else jnp.zeros(acc.shape, F32)
-    outer, rows, _ = out.shape
-    tile = min(256, rows)
-    tile = 128 if rows % 256 else tile
-    tiles = [(h, b) for h in range(outer) for b in range(0, rows, tile)]
-
-    def merge(low, low_begin, high, high_begin):
-        for h, b in tiles:
-            total = dot(read(low, h, low_begin + b, tile), mix[pair, pair])
-            total += dot(read(high, h, high_begin + b, tile), mix[pair, 1 - pair])
-            out[h, b : b + tile, :] = total.astype(BF16)
-
-    pl.when(bit0 != bit1)(lambda: merge([left], begin, [keep], begin))
-    pl.when(bit0 == bit1)(lambda: merge(risen, begin, [passed], 0))
+    outer, total_rows, _ = out.shape
+
+    def merge(outer_of, inner_of):
+        at = 0
+        for k, (skip, rows) in enumerate(segments):
+            for h in range(outer):
+                total = dot(outer_of(k, h, skip, rows, at), mix[pair, pair])
+                total += dot(inner_of(k, h, skip, rows, at), mix[pair, 1 - pair])
+                out[h, at : at + rows, :] = total.astype(BF16)
+            at += rows
+
+    def near():
+        merge(
+            lambda k, h, skip, rows, at: left[k][h, skip : skip + rows, :],
+            lambda k, h, skip, rows, at: keep[h, begin + at : begin + at + rows, :],
+        )
+
+    def distant():
+        merge(
+            lambda k, h, skip, rows, at: risen[h, at : at + rows, :],
+            lambda k, h, skip, rows, at: passed[k][h, skip : skip + rows, :],
+        )
+
+    pl.when(bit0 != bit1)(near)
+    pl.when(bit0 == bit1)(distant)
 
     def add(flip):
         for h in range(outer):
-            both = (own[h, begin : begin + rows, :], out[h])
+            both = (own[h, begin : begin + total_rows, :], out[h])
             acc[...] += dot_t(both[flip], both[1 - flip])
 
     pl.when(bit1 == 0)(lambda: add(0))
     pl.when(bit1 == 1)(lambda: add(1))
-    if last:
+    if chained:
         write_halves(ids[0], acc, *outs)
     else:
         outs[0][...] = acc[...]
 
 
-def merge_other(ids, mix, own, begin, left, keep, passed, risen, start):
-    width = own.shape[-1]
+def merge_other(begin, segments, start, ids, mix, own, keep, risen, left, passed):
+    outer, _, width = own.shape
     chained = start is not None
     outs = halves(width) if chained else [shape((width, width), F32)]
-    args = [ids, mix, own, left, keep, passed] + ([start] if chained else []) + risen
-    return call(
-        functools.partial(merge_other_kernel, begin, chained, chained), 12,
-        [SMEM] + [VMEM] * (len(args) - 1), [shape(passed.shape, BF16)] + outs,
+    args = [ids, mix, own, keep, risen, *left, *passed] + ([start] if chained else [])
+    rows = sum(size for _, size in segments)
+    return call(
+        functools.partial(merge_other_kernel, begin, segments, chained), 12,
+        [SMEM] + [VMEM] * (len(args) - 1), [shape((outer, rows, width), BF16)] + outs,
         [pltpu.VMEM((width, width), F32)], *args,
     )
 
@@ -394,7 +409,7 @@
                 total += dot(read(high, h, b, tile), mix[width:])
                 out[h, b : b + tile, :] = total.astype(BF16)
 
-    tile = min(256, *(other.shape[1] & -other.shape[1] for other in others))
+    tile = math.gcd(256, *(other.shape[1] for other in others))
     pl.when(bit == 0)(lambda: finish([own], others))
     pl.when(bit == 1)(lambda: finish(others, [own]))
     if not last:
@@ -427,7 +442,7 @@
     block_rows = rows // groups
     cut = block_rows * 3 // 4
     tail = block_rows - cut
-    part = block_rows // 2
+    part = block_rows * 7 // 16
 
     middle, forward, rise, leave = [], [], [], []
     for base in range(0, groups, 4):
@@ -437,11 +452,12 @@
         leave += [(base, base + 2), (base + 3, base + 1)]
     pair = [(i, i ^ 1) for i in range(groups)]
 
-    far_own, across = pick(snapshot_basis, 59, [(1, 1, 0, block_rows), (1, 0, 0, block_rows)])
+    far_own, across = pick(snapshot_basis, 48, [(1, 1, 0, block_rows), (1, 0, 0, block_rows)])
     far = send(far_own, pair)
     pass_on = send(across, middle)
-    cuts = [(0, 1, 0, cut), (0, 1, cut, tail), (0, 0, 0, block_rows)]
-    near_own, tail_own, mine = pick(after(snapshot_basis, far_own), 59, cuts)
+    cuts = [(0, 1, 0, cut), (0, 1, cut, tail), (0, 0, 0, block_rows), (1, 0, 0, cut),
+            (1, 0, cut, tail)]
+    near_own, tail_own, mine, leave_head, leave_tail = pick(after(snapshot_basis, far_own), 48, cuts)
 
     own_halves = own_gram(ids, [far_own, across, near_own, tail_own, mine])
     own_sum = scatter_space(ids, *own_halves)
@@ -464,25 +480,28 @@
     cross = cross_gram(ids, mine, near_head, 0, cross, False)[0]
     cross_halves = cross_gram(ids, mine, near_tail, cut, cross, True)
     cross_sum = scatter_space(ids, *cross_halves)
-    here = cross_sum + send(cross_sum, pair)
-    there = swap(here, "group", 2)
+    one, two, three = [swap(cross_sum, "group", k) for k in (1, 2, 3)]
+    here = cross_sum + one
+    there = two + three
     both = jnp.stack([jnp.where(bit1 == 0, here, there), jnp.where(bit1 == 0, there, here)])
 
     pass_parts = divide(pass_on, cut)
-    pass_head = send(after(pass_parts[0], here), forward)
-    left = send(after(across, here), leave)
-    rise_tail = send(after(far_tail, here), rise)
-    pass_tail = send(after(pass_parts[1], here), forward)
+    left_head = send(after(leave_head, cross_sum), leave)
+    pass_head = send(after(pass_parts[0], cross_sum), forward)
+    rise_tail = send(after(far_tail, cross_sum), rise)
+    left_tail = send(after(leave_tail, cross_sum), leave)
+    pass_tail = send(after(pass_parts[1], cross_sum), forward)
 
     mix, gram = pair_filter(ids, diag, gather_space(both), sketch)
     diag = next_diag(gram, mix)
     own_merged = merge_own(ids, mix, mine, near_head, near_tail)
+    args = [ids, mix, own_merged, keep]
     other_head, cross = merge_other(
-        ids, mix, own_merged, 0, left, keep, pass_head, [rise_head, rise_tail], None
+        0, [(0, part)], None, *args, rise_head, [left_head], [pass_head]
     )
     other_tail, *both_halves = merge_other(
-        ids, mix, own_merged, cut, left, keep, pass_tail, [rise_head, rise_tail],
-        cross,
+        part, [(part, cut - part), (0, tail)], cross, *args, rise_tail,
+        [left_head, left_tail], [pass_head, pass_tail],
     )
     total = scatter_space(ids, *both_halves)
     one, two, three = [swap(total, "group", k) for k in (1, 2, 3)]

time: 197 us -> 186 us (0.944)
  waiting for transfers between devices: 89 us -> 72.7 us
  starting transfers between devices: 55.5 us -> 61.5 us
    ppermute x11, waiting for transfers between devices: 40 us -> 11.2 us  [send(): return lax.ppermute(value, 'group', routes)]
    ppermute x40 -> x42, waiting for transfers between devices: 49 us -> 61.4 us  [swap(): return lax.ppermute(block, axis, [(i, i ^ offset) for i in range(count)])]
    ppermute x40 -> x42, starting transfers between devices: 33.2 us -> 38.7 us  [swap(): return lax.ppermute(block, axis, [(i, i ^ offset) for i in range(count)])]
    unnamed x28 -> x22, local copies, waits for them, and re-layouts: 8.11 us -> 6.27 us
  transfers between devices with their start and end apart: 51 -> 53, of which waited for: 26 -> 26; matrix products, arithmetic and copies ran while one was open for 1% -> 1% of each run, Pallas kernels for 11% -> 12%
where the time goes in v1:
time: 186 us; the launch traced here: 185 us
  waiting for transfers between devices  72.7 us (39%)
  starting transfers between devices  61.5 us (33%)
  Pallas kernels  42.4 us (23%)
  local copies, waits for them, and re-layouts  6.3 us (3%)
    ppermute x42, waiting for transfers between devices, swap(): return lax.ppermute(block, axis, [(i, i ^ offset) for i in range(count)])  61.4 us
    pallas_call x18, Pallas kernels, call(): pl.pallas_call(kernel, in_specs=in_specs, out_specs=[VMEM] * len(outs), o...  42.4 us
    ppermute x42, starting transfers between devices, swap(): return lax.ppermute(block, axis, [(i, i ^ offset) for i in range(count)])  38.7 us
    ppermute x11, starting transfers between devices, send(): return lax.ppermute(value, 'group', routes)  22.8 us
    ppermute x11, waiting for transfers between devices, send(): return lax.ppermute(value, 'group', routes)  11.2 us
    unnamed x22, local copies, waits for them, and re-layouts  6.27 us
  transfers between devices with their start and end apart: 53, of which 26 were waited for; matrix products, arithmetic and copies ran while one was open for 1% of the time, Pallas kernels for 12%

profile of v1, /device:TPU:0, one launch (start us, length us, event | category | flops | bytes accessed | tf_op | source)
XLA Modules:
  0.0 184.9 jit_solution(3786761096474273410)
XLA Ops:
  0.0 2.5 %shard_map.28 = (bf16[1,2048,256]{2,1,0:T(8,128)(2,1)}, bf16[1,2048,256]{2,1,0:T(8,128)(2,1)S(1)}) custom-call(bf16[8192,256]{1,0:T(8,128)(2,1)} %x_ref.2), custom_call_target="tpu_custom_call" | custom-call | tf_op jit(solution)/shard_map/pallas_call | solution.py:57
  2.5 2.9 %shard_map.29 = (bf16[1,1536,256]{2,1,0:T(8,128)(2,1)}, bf16[1,512,256]{2,1,0:T(8,128)(2,1)}, bf16[1,2048,256]{2,1,0:T(8,128)(2,1)S(1)}, bf16[1,1536,256]{2,1,0:T(8,128)(2,1)S(1)}, bf16[1,512,256]{2,1,0:T(8,128)(2,1)S(1)}) custom-call(bf16[8192,256]{1,0:T(8,128)(2,1)} %x_ref.2), custom_call_target="tpu_custom_call" | custom-call | tf_op jit(solution)/shard_map/pallas_call | solution.py:57
  6.2 3.1 %shard_map.30 = (f32[128,256]{1,0:T(8,128)S(1)}, f32[128,256]{1,0:T(8,128)S(1)}) custom-call(s32[3]{0:T(128)S(1)} %pad_add_fusion.ids, bf16[1,2048,256]{2,1,0:T(8,128)(2,1)} %get-tuple-element.71.refs_0_, bf16[1,2048,256]{2,1,0:T(8,128)(2,1)S(1)} %get-tuple-element.50.refs_1_.own, bf16[1,1536,256]{2,1,0:T(8,128)(2,1)} %get-tuple-element.62.refs_2_, ...), custom_call_target="tpu_custom_call" | custom-call | tf_op jit(solution)/shard_map/pallas_call | solution.py:57
  9.8 2.6 %collective-permute-start.16 = (bf16[1,2048,256]{2,1,0:T(8,128)(2,1)}, bf16[1,2048,256]{2,1,0:T(8,128)(2,1)S(1)}, u32[]{:S(2)}, u32[]{:S(2)}) collective-permute-start(bf16[1,2048,256]{2,1,0:T(8,128)(2,1)} %get-tuple-element.71.refs_0_), channel_id=1, source_target_pairs={{0,1},{1,0},{2,3},{3,2},{4,5},{5,4},{6,7},{7,6},{8,9},{9,8},{10,11... | collective-permute-start | bytes 3145736 | tf_op jit(solution)/shard_map/ppermute | solution.py:26
  18.5 2.4 %collective-permute-done.3 = f32[32,256]{1,0:T(8,128)S(1)} collective-permute-done((f32[32,256]{1,0:T(8,128)S(1)}, f32[32,256]{1,0:T(8,128)S(1)}, u32[]{:S(2)}, u32[]{:S(2)}) %collective-permute-start.3) | collective-permute-done | bytes 32800 | tf_op jit(solution)/shard_map/ppermute | solution.py:22
  23.9 2.8 %collective-permute-start.6 = (f32[32,256]{1,0:T(8,128)S(1)}, f32[32,256]{1,0:T(8,128)S(1)}, u32[]{:S(2)}, u32[]{:S(2)}) collective-permute-start(f32[32,256]{1,0:T(8,128)S(1)} %add_add_fusion.2), channel_id=1, source_target_pairs={{0,3},{1,2},{2,1},{3,0},{4,7},{5,6},{6,5},{7,4},{8,11},{9,10},{10,... | collective-permute-start | bytes 98312 | tf_op jit(solution)/shard_map/ppermute | solution.py:22
  26.7 2.2 %collective-permute-start.5 = (f32[32,256]{1,0:T(8,128)S(1)}, f32[32,256]{1,0:T(8,128)S(1)}, u32[]{:S(2)}, u32[]{:S(2)}) collective-permute-start(f32[32,256]{1,0:T(8,128)S(1)} %add_add_fusion.2), channel_id=1, source_target_pairs={{0,2},{1,3},{2,0},{3,1},{4,6},{5,7},{6,4},{7,5},{8,10},{9,11},{10,... | collective-permute-start | bytes 98312 | tf_op jit(solution)/shard_map/ppermute | solution.py:22
  28.9 27.7 %collective-permute-done.6 = f32[32,256]{1,0:T(8,128)S(1)} collective-permute-done((f32[32,256]{1,0:T(8,128)S(1)}, f32[32,256]{1,0:T(8,128)S(1)}, u32[]{:S(2)}, u32[]{:S(2)}) %collective-permute-start.6) | collective-permute-done | bytes 32800 | tf_op jit(solution)/shard_map/ppermute | solution.py:22
  56.5 2.0 %collective-permute-start.14 = (bf16[1,512,256]{2,1,0:T(8,128)(2,1)}, bf16[1,512,256]{2,1,0:T(8,128)(2,1)S(1)}, u32[]{:S(2)}, u32[]{:S(2)}) collective-permute-start(bf16[1,512,256]{2,1,0:T(8,128)(2,1)} %get-tuple-element.61.refs_3_), channel_id=1, source_target_pairs={{0,1},{1,0},{2,3},{3,2},{4,5},{5,4},{6,7},{7,6},{8,9},{9,8},{10,11... | collective-permute-start | bytes 786440 | tf_op jit(solution)/shard_map/ppermute | solution.py:26
  58.6 2.2 %collective-permute-done.4 = f32[32,256]{1,0:T(8,128)S(1)} collective-permute-done((f32[32,256]{1,0:T(8,128)S(1)}, f32[32,256]{1,0:T(8,128)S(1)}, u32[]{:S(2)}, u32[]{:S(2)}) %collective-permute-start.4) | collective-permute-done | bytes 32800 | tf_op jit(solution)/shard_map/ppermute | solution.py:22
  67.2 2.5 %collective-permute-start.12 = (f32[4,32,256]{2,1,0:T(8,128)S(1)}, f32[4,32,256]{2,1,0:T(8,128)}, u32[]{:S(2)}, u32[]{:S(2)}) collective-permute-start(f32[4,32,256]{2,1,0:T(8,128)S(1)} %pad_maximum_fusion.1.refs_0_), channel_id=1, source_target_pairs={{0,24},{4,28},{8,16},{12,20},{16,8},{20,12},{24,0},{28,4},{1,25},{... | collective-permute-start | bytes 393224 | tf_op jit(solution)/shard_map/ppermute | solution.py:22
  71.4 2.9 %collective-permute-done.12.refs_6_ = f32[4,32,256]{2,1,0:T(8,128)} collective-permute-done((f32[4,32,256]{2,1,0:T(8,128)S(1)}, f32[4,32,256]{2,1,0:T(8,128)}, u32[]{:S(2)}, u32[]{:S(2)}) %collective-permute-start.12) | collective-permute-done | bytes 131104 | tf_op jit(solution)/shard_map/ppermute | solution.py:22
  79.9 1.9 %collective-permute-done.20 = f32[32,256]{1,0:T(8,128)S(1)} collective-permute-done((f32[32,256]{1,0:T(8,128)S(1)}, f32[32,256]{1,0:T(8,128)S(1)}, u32[]{:S(2)}, u32[]{:S(2)}) %collective-permute-start.20) | collective-permute-done | bytes 32800 | tf_op jit(solution)/shard_map/ppermute | solution.py:22
  87.0 2.0 %collective-permute-start.21 = (f32[32,256]{1,0:T(8,128)}, f32[32,256]{1,0:T(8,128)S(1)}, u32[]{:S(2)}, u32[]{:S(2)}) collective-permute-start(f32[32,256]{1,0:T(8,128)} %add_add_fusion.1), channel_id=1, source_target_pairs={{0,1},{1,0},{2,3},{3,2},{4,5},{5,4},{6,7},{7,6},{8,9},{9,8},{10,11... | collective-permute-start | bytes 98312 | tf_op jit(solution)/shard_map/ppermute | solution.py:22
  92.2 2.9 %collective-permute-start.33 = (bf16[1,1536,256]{2,1,0:T(8,128)(2,1)}, bf16[1,1536,256]{2,1,0:T(8,128)(2,1)S(1)}, u32[]{:S(2)}, u32[]{:S(2)}) collective-permute-start(bf16[1,1536,256]{2,1,0:T(8,128)(2,1)} %copy-done.9), channel_id=1, source_target_pairs={{0,2},{3,1},{4,6},{7,5},{8,10},{11,9},{12,14},{15,13},{16,18},{19,... | collective-permute-start | bytes 2359304 | tf_op jit(solution)/shard_map/ppermute | solution.py:26
  101.3 2.4 %collective-permute-done.29.refs_6_ = f32[2,32,256]{2,1,0:T(8,128)S(1)} collective-permute-done((f32[2,32,256]{2,1,0:T(8,128)S(1)}, f32[2,32,256]{2,1,0:T(8,128)S(1)}, u32[]{:S(2)}, u32[]{:S(2)}) %collective-permute-start.29) | collective-permute-done | bytes 65568 | tf_op jit(solution)/shard_map/ppermute | solution.py:22
  113.1 5.5 %collective-permute-start.37 = (bf16[1,512,256]{2,1,0:T(8,128)(2,1)}, bf16[1,512,256]{2,1,0:T(8,128)(2,1)S(1)}, u32[]{:S(2)}, u32[]{:S(2)}) collective-permute-start(bf16[1,512,256]{2,1,0:T(8,128)(2,1)} %copy-done.10), channel_id=1, source_target_pairs={{0,2},{3,1},{4,6},{7,5},{8,10},{11,9},{12,14},{15,13},{16,18},{19,... | collective-permute-start | bytes 786440 | tf_op jit(solution)/shard_map/ppermute | solution.py:26
  118.6 11.2 %collective-permute-done.32.risen = bf16[1,896,256]{2,1,0:T(8,128)(2,1)S(1)} collective-permute-done((bf16[1,896,256]{2,1,0:T(8,128)(2,1)S(1)}, bf16[1,896,256]{2,1,0:T(8,128)(2,1)S(1)}, u32[]{:S(2)}, u32[]{:S(2)}) %collective-permute-start.32) | collective-permute-done | bytes 458784 | tf_op jit(solution)/shard_map/ppermute | solution.py:26
  134.8 9.8 %shard_map.37 = (bf16[2,2,256,256]{3,2,1,0:T(8,128)(2,1)S(1)}, f32[2,512,512]{2,1,0:T(8,128)S(1)}) custom-call(s32[3]{0:T(128)S(1)} %pad_add_fusion.ids, f32[4,256,256]{2,1,0:T(8,128)S(1)} %shard_map.32.diag, f32[2,512,256]{2,1,0:T(8,128)S(1)} %copy-done, f32[2,32,256]{2,1,0:T(8,128)S(1)} %pad_maximum_fusion.2.refs_0_, ...), custom_call_target="tpu_custom_call" | custom-call | tf_op jit(solution)/shard_map/pallas_call | solution.py:57
  146.5 2.2 %shard_map.42 = (bf16[1,896,256]{2,1,0:T(8,128)(2,1)S(1)}, f32[256,256]{1,0:T(8,128)S(1)}) custom-call(s32[3]{0:T(128)S(1)} %pad_add_fusion.ids, bf16[2,2,256,256]{3,2,1,0:T(8,128)(2,1)S(1)} %get-tuple-element.70.mix, bf16[1,2048,256]{2,1,0:T(8,128)(2,1)S(1)} %shard_map.39.own, bf16[1,2048,256]{2,1,0:T(8,128)(2,1)} %collective-permute-done.31.keep, ...), custom_call_target="tpu_custom_call" | custom-call | tf_op jit(solution)/shard_map/pallas_call | solution.py:57
  148.8 2.1 %shard_map.43 = (bf16[1,1152,256]{2,1,0:T(8,128)(2,1)S(1)}, f32[128,256]{1,0:T(8,128)S(1)}, f32[128,256]{1,0:T(8,128)S(1)}) custom-call(s32[3]{0:T(128)S(1)} %pad_add_fusion.ids, bf16[2,2,256,256]{3,2,1,0:T(8,128)(2,1)S(1)} %get-tuple-element.70.mix, bf16[1,2048,256]{2,1,0:T(8,128)(2,1)S(1)} %shard_map.39.own, ...), custom_call_target="tpu_custom_call" | custom-call | tf_op jit(solution)/shard_map/pallas_call | solution.py:57
  159.8 2.4 %collective-permute-start.45 = (f32[32,256]{1,0:T(8,128)S(1)}, f32[32,256]{1,0:T(8,128)S(1)}, u32[]{:S(2)}, u32[]{:S(2)}) collective-permute-start(f32[32,256]{1,0:T(8,128)S(1)} %add_add_fusion), channel_id=1, source_target_pairs={{0,3},{1,2},{2,1},{3,0},{4,7},{5,6},{6,5},{7,4},{8,11},{9,10},{10,... | collective-permute-start | bytes 98312 | tf_op jit(solution)/shard_map/ppermute | solution.py:22
  174.5 1.9 %shard_map.38.diag = f32[2,256,256]{2,1,0:T(8,128)S(1)} custom-call(f32[2,512,512]{2,1,0:T(8,128)S(1)} %get-tuple-element.69.gram, bf16[2,2,256,256]{3,2,1,0:T(8,128)(2,1)S(1)} %get-tuple-element.70.mix), custom_call_target="tpu_custom_call" | custom-call | tf_op jit(solution)/shard_map/pallas_call | solution.py:57
  176.4 8.4 %shard_map.45 = bf16[1,2048,256]{2,1,0:T(8,128)(2,1)} custom-call(s32[3]{0:T(128)S(1)} %pad_add_fusion.ids, f32[2,256,256]{2,1,0:T(8,128)S(1)} %shard_map.38.diag, f32[2,512,256]{2,1,0:T(8,128)S(1)} %copy-done, bf16[1,2048,256]{2,1,0:T(8,128)(2,1)S(1)} %shard_map.39.own, bf16[1,896,256]{2,1,0:T(8,128)(2,1)S(1)} %get-tuple-element.78.refs_0_, ...), custom_call_target="tpu_custom_call" | custom-call | tf_op jit(solution)/shard_map/pallas_call | solution.py:57
  (132 shorter events, 75.8 us)
Async XLA Ops:
  9.8 52.7 %collective-permute-start.16 = (bf16[1,2048,256]{2,1,0:T(8,128)(2,1)}, bf16[1,2048,256]{2,1,0:T(8,128)(2,1)S(1)}, u32[]{:S(2)}, u32[]{:S(2)}) collective-permute-start(bf16[1,2048,256]{2,1,0:T(8,128)(2,1)} %get-tuple-element.71.refs_0_), channel_id=1, source_target_pairs={{0,1},{1,0},{2,3},{3,2},{4,5},{5,4},{6,7},{7,6},{8,9},{9,8},{10,11... | collective-permute-start | bytes 3145736 | tf_op jit(solution)/shard_map/ppermute | solution.py:26
  20.9 43.6 %collective-permute-start.15 = (bf16[1,1536,256]{2,1,0:T(8,128)(2,1)}, bf16[1,1536,256]{2,1,0:T(8,128)(2,1)}, u32[]{:S(2)}, u32[]{:S(2)}) collective-permute-start(bf16[1,1536,256]{2,1,0:T(8,128)(2,1)} %get-tuple-element.62.refs_2_), channel_id=1, source_target_pairs={{0,1},{1,0},{2,3},{3,2},{4,5},{5,4},{6,7},{7,6},{8,9},{9,8},{10,11... | collective-permute-start | bytes 2359304 | tf_op jit(solution)/shard_map/ppermute | solution.py:26
  22.3 64.7 %collective-permute-start.34 = (bf16[1,2048,256]{2,1,0:T(8,128)(2,1)S(1)}, bf16[1,2048,256]{2,1,0:T(8,128)(2,1)}, u32[]{:S(2)}, u32[]{:S(2)}) collective-permute-start(bf16[1,2048,256]{2,1,0:T(8,128)(2,1)S(1)} %get-tuple-element.50.refs_1_.own), channel_id=1, source_target_pairs={{1,2},{2,1},{5,6},{6,5},{9,10},{10,9},{13,14},{14,13},{17,18},{18,... | collective-permute-start | bytes 3145736 | tf_op jit(solution)/shard_map/ppermute | solution.py:26
  23.9 32.6 %collective-permute-start.6 = (f32[32,256]{1,0:T(8,128)S(1)}, f32[32,256]{1,0:T(8,128)S(1)}, u32[]{:S(2)}, u32[]{:S(2)}) collective-permute-start(f32[32,256]{1,0:T(8,128)S(1)} %add_add_fusion.2), channel_id=1, source_target_pairs={{0,3},{1,2},{2,1},{3,0},{4,7},{5,6},{6,5},{7,4},{8,11},{9,10},{10,... | collective-permute-start | bytes 98312 | tf_op jit(solution)/shard_map/ppermute | solution.py:22
  26.7 29.8 %collective-permute-start.5 = (f32[32,256]{1,0:T(8,128)S(1)}, f32[32,256]{1,0:T(8,128)S(1)}, u32[]{:S(2)}, u32[]{:S(2)}) collective-permute-start(f32[32,256]{1,0:T(8,128)S(1)} %add_add_fusion.2), channel_id=1, source_target_pairs={{0,2},{1,3},{2,0},{3,1},{4,6},{5,7},{6,4},{7,5},{8,10},{9,11},{10,... | collective-permute-start | bytes 98312 | tf_op jit(solution)/shard_map/ppermute | solution.py:22
  56.5 9.7 %collective-permute-start.14 = (bf16[1,512,256]{2,1,0:T(8,128)(2,1)}, bf16[1,512,256]{2,1,0:T(8,128)(2,1)S(1)}, u32[]{:S(2)}, u32[]{:S(2)}) collective-permute-start(bf16[1,512,256]{2,1,0:T(8,128)(2,1)} %get-tuple-element.61.refs_3_), channel_id=1, source_target_pairs={{0,1},{1,0},{2,3},{3,2},{4,5},{5,4},{6,7},{7,6},{8,9},{9,8},{10,11... | collective-permute-start | bytes 786440 | tf_op jit(solution)/shard_map/ppermute | solution.py:26
  60.8 39.3 %collective-permute-start.31 = (bf16[1,2048,256]{2,1,0:T(8,128)(2,1)}, bf16[1,2048,256]{2,1,0:T(8,128)(2,1)}, u32[]{:S(2)}, u32[]{:S(2)}) collective-permute-start(bf16[1,2048,256]{2,1,0:T(8,128)(2,1)} %get-tuple-element.71.refs_0_), channel_id=1, source_target_pairs={{1,2},{2,1},{5,6},{6,5},{9,10},{10,9},{13,14},{14,13},{17,18},{18,... | collective-permute-start | bytes 3145736 | tf_op jit(solution)/shard_map/ppermute | solution.py:26
  67.2 7.1 %collective-permute-start.12 = (f32[4,32,256]{2,1,0:T(8,128)S(1)}, f32[4,32,256]{2,1,0:T(8,128)}, u32[]{:S(2)}, u32[]{:S(2)}) collective-permute-start(f32[4,32,256]{2,1,0:T(8,128)S(1)} %pad_maximum_fusion.1.refs_0_), channel_id=1, source_target_pairs={{0,24},{4,28},{8,16},{12,20},{16,8},{20,12},{24,0},{28,4},{1,25},{... | collective-permute-start | bytes 393224 | tf_op jit(solution)/shard_map/ppermute | solution.py:22
  69.7 7.2 %collective-permute-start.10 = (f32[4,32,256]{2,1,0:T(8,128)S(1)}, f32[4,32,256]{2,1,0:T(8,128)S(1)}, u32[]{:S(2)}, u32[]{:S(2)}) collective-permute-start(f32[4,32,256]{2,1,0:T(8,128)S(1)} %pad_maximum_fusion.1.refs_0_), channel_id=1, source_target_pairs={{0,16},{4,20},{8,24},{12,28},{16,0},{20,4},{24,8},{28,12},{1,17},{... | collective-permute-start | bytes 393224 | tf_op jit(solution)/shard_map/ppermute | solution.py:22
  70.8 7.8 %collective-permute-start.18 = (f32[32,256]{1,0:T(8,128)S(1)}, f32[32,256]{1,0:T(8,128)S(1)}, u32[]{:S(2)}, u32[]{:S(2)}) collective-permute-start(f32[32,256]{1,0:T(8,128)S(1)} %get-tuple-element.66), channel_id=1, source_target_pairs={{0,8},{4,12},{8,0},{12,4},{16,24},{20,28},{24,16},{28,20},{1,9},{5... | collective-permute-start | bytes 98312 | tf_op jit(solution)/shard_map/ppermute | solution.py:22
  74.3 5.7 %collective-permute-start.19 = (f32[32,256]{1,0:T(8,128)S(1)}, f32[32,256]{1,0:T(8,128)S(1)}, u32[]{:S(2)}, u32[]{:S(2)}) collective-permute-start(f32[32,256]{1,0:T(8,128)S(1)} %get-tuple-element.67), channel_id=1, source_target_pairs={{0,16},{4,20},{8,24},{12,28},{16,0},{20,4},{24,8},{28,12},{1,17},{... | collective-permute-start | bytes 98312 | tf_op jit(solution)/shard_map/ppermute | solution.py:22
  81.9 9.7 %collective-permute-start.13 = (f32[4,32,256]{2,1,0:T(8,128)}, f32[4,32,256]{2,1,0:T(8,128)}, u32[]{:S(2)}, u32[]{:S(2)}) collective-permute-start(f32[4,32,256]{2,1,0:T(8,128)} %collective-permute-done.12.refs_6_), channel_id=1, source_target_pairs={{0,4},{4,0},{8,12},{12,8},{16,20},{20,16},{24,28},{28,24},{1,5},{5... | collective-permute-start | bytes 393224 | tf_op jit(solution)/shard_map/ppermute | solution.py:22
  84.0 7.7 %collective-permute-start.23 = (f32[32,256]{1,0:T(8,128)}, f32[32,256]{1,0:T(8,128)}, u32[]{:S(2)}, u32[]{:S(2)}) collective-permute-start(f32[32,256]{1,0:T(8,128)} %add_add_fusion.1), channel_id=1, source_target_pairs={{0,3},{1,2},{2,1},{3,0},{4,7},{5,6},{6,5},{7,4},{8,11},{9,10},{10,... | collective-permute-start | bytes 98312 | tf_op jit(solution)/shard_map/ppermute | solution.py:22
  86.1 6.1 %collective-permute-start.22 = (f32[32,256]{1,0:T(8,128)}, f32[32,256]{1,0:T(8,128)}, u32[]{:S(2)}, u32[]{:S(2)}) collective-permute-start(f32[32,256]{1,0:T(8,128)} %add_add_fusion.1), channel_id=1, source_target_pairs={{0,2},{1,3},{2,0},{3,1},{4,6},{5,7},{6,4},{7,5},{8,10},{9,11},{10,... | collective-permute-start | bytes 98312 | tf_op jit(solution)/shard_map/ppermute | solution.py:22
  87.0 8.1 %collective-permute-start.21 = (f32[32,256]{1,0:T(8,128)}, f32[32,256]{1,0:T(8,128)S(1)}, u32[]{:S(2)}, u32[]{:S(2)}) collective-permute-start(f32[32,256]{1,0:T(8,128)} %add_add_fusion.1), channel_id=1, source_target_pairs={{0,1},{1,0},{2,3},{3,2},{4,5},{5,4},{6,7},{7,6},{8,9},{9,8},{10,11... | collective-permute-start | bytes 98312 | tf_op jit(solution)/shard_map/ppermute | solution.py:22
  91.6 5.6 %collective-permute-start.11 = (f32[4,32,256]{2,1,0:T(8,128)}, f32[4,32,256]{2,1,0:T(8,128)S(1)}, u32[]{:S(2)}, u32[]{:S(2)}) collective-permute-start(f32[4,32,256]{2,1,0:T(8,128)} %copy-done.3), channel_id=1, source_target_pairs={{0,4},{4,0},{8,12},{12,8},{16,20},{20,16},{24,28},{28,24},{1,5},{5... | collective-permute-start | bytes 393224 | tf_op jit(solution)/shard_map/ppermute | solution.py:22
  91.7 6.8 %collective-permute-start.9 = (f32[4,32,256]{2,1,0:T(8,128)}, f32[4,32,256]{2,1,0:T(8,128)S(1)}, u32[]{:S(2)}, u32[]{:S(2)}) collective-permute-start(f32[4,32,256]{2,1,0:T(8,128)} %copy-done.5), channel_id=1, source_target_pairs={{0,4},{4,0},{8,12},{12,8},{16,20},{20,16},{24,28},{28,24},{1,5},{5... | collective-permute-start | bytes 393224 | tf_op jit(solution)/shard_map/ppermute | solution.py:22
  92.2 54.3 %collective-permute-start.33 = (bf16[1,1536,256]{2,1,0:T(8,128)(2,1)}, bf16[1,1536,256]{2,1,0:T(8,128)(2,1)S(1)}, u32[]{:S(2)}, u32[]{:S(2)}) collective-permute-start(bf16[1,1536,256]{2,1,0:T(8,128)(2,1)} %copy-done.9), channel_id=1, source_target_pairs={{0,2},{3,1},{4,6},{7,5},{8,10},{11,9},{12,14},{15,13},{16,18},{19,... | collective-permute-start | bytes 2359304 | tf_op jit(solution)/shard_map/ppermute | solution.py:26
  95.1 51.4 %collective-permute-start.35 = (bf16[1,1536,256]{2,1,0:T(8,128)(2,1)S(1)}, bf16[1,1536,256]{2,1,0:T(8,128)(2,1)S(1)}, u32[]{:S(2)}, u32[]{:S(2)}) collective-permute-start(bf16[1,1536,256]{2,1,0:T(8,128)(2,1)S(1)} %get-tuple-element.77), channel_id=1, source_target_pairs={{1,0},{2,3},{5,4},{6,7},{9,8},{10,11},{13,12},{14,15},{17,16},{18,... | collective-permute-start | bytes 2359304 | tf_op jit(solution)/shard_map/ppermute | solution.py:26
  97.2 32.6 %collective-permute-start.32 = (bf16[1,896,256]{2,1,0:T(8,128)(2,1)S(1)}, bf16[1,896,256]{2,1,0:T(8,128)(2,1)S(1)}, u32[]{:S(2)}, u32[]{:S(2)}) collective-permute-start(bf16[1,896,256]{2,1,0:T(8,128)(2,1)S(1)} %get-tuple-element.73), channel_id=1, source_target_pairs={{1,3},{2,0},{5,7},{6,4},{9,11},{10,8},{13,15},{14,12},{17,19},{18,... | collective-permute-start | bytes 1376264 | tf_op jit(solution)/shard_map/ppermute | solution.py:26
  105.0 43.7 %collective-permute-start.36 = (bf16[1,1152,256]{2,1,0:T(8,128)(2,1)S(1)}, bf16[1,1152,256]{2,1,0:T(8,128)(2,1)S(1)}, u32[]{:S(2)}, u32[]{:S(2)}) collective-permute-start(bf16[1,1152,256]{2,1,0:T(8,128)(2,1)S(1)} %get-tuple-element.80), channel_id=1, source_target_pairs={{1,3},{2,0},{5,7},{6,4},{9,11},{10,8},{13,15},{14,12},{17,19},{18,... | collective-permute-start | bytes 1769480 | tf_op jit(solution)/shard_map/ppermute | solution.py:26
  113.1 35.7 %collective-permute-start.37 = (bf16[1,512,256]{2,1,0:T(8,128)(2,1)}, bf16[1,512,256]{2,1,0:T(8,128)(2,1)S(1)}, u32[]{:S(2)}, u32[]{:S(2)}) collective-permute-start(bf16[1,512,256]{2,1,0:T(8,128)(2,1)} %copy-done.10), channel_id=1, source_target_pairs={{0,2},{3,1},{4,6},{7,5},{8,10},{11,9},{12,14},{15,13},{16,18},{19,... | collective-permute-start | bytes 786440 | tf_op jit(solution)/shard_map/ppermute | solution.py:26
  129.8 19.0 %collective-permute-start.38 = (bf16[1,512,256]{2,1,0:T(8,128)(2,1)S(1)}, bf16[1,512,256]{2,1,0:T(8,128)(2,1)S(1)}, u32[]{:S(2)}, u32[]{:S(2)}) collective-permute-start(bf16[1,512,256]{2,1,0:T(8,128)(2,1)S(1)} %get-tuple-element.84), channel_id=1, source_target_pairs={{1,0},{2,3},{5,4},{6,7},{9,8},{10,11},{13,12},{14,15},{17,16},{18,... | collective-permute-start | bytes 786440 | tf_op jit(solution)/shard_map/ppermute | solution.py:26
  159.8 6.1 %collective-permute-start.45 = (f32[32,256]{1,0:T(8,128)S(1)}, f32[32,256]{1,0:T(8,128)S(1)}, u32[]{:S(2)}, u32[]{:S(2)}) collective-permute-start(f32[32,256]{1,0:T(8,128)S(1)} %add_add_fusion), channel_id=1, source_target_pairs={{0,3},{1,2},{2,1},{3,0},{4,7},{5,6},{6,5},{7,4},{8,11},{9,10},{10,... | collective-permute-start | bytes 98312 | tf_op jit(solution)/shard_map/ppermute | solution.py:22
  (40 other events, 241.0 us)

commit v2 on v1

--- a/solution.py
+++ b/solution.py
@@ -13,7 +13,6 @@
 F32 = jnp.float32
 BF16 = jnp.bfloat16
 HBM = pl.BlockSpec(memory_space=pltpu.HBM)
-SMEM = pl.BlockSpec(memory_space=pltpu.SMEM)
 VMEM = pl.BlockSpec(memory_space=pltpu.VMEM)
 
 
@@ -98,13 +97,19 @@
     )
 
 
-def place(me, offset, rows, width):
-    device = jnp.bitwise_xor(me, offset)
+def place(offset, rows, width):
+    device = jnp.bitwise_xor(where()[0], offset)
     start = (device & 1) * (width // 2) + (device >> 1) * rows
     return pl.multiple_of(start, rows)
 
 
-def write_halves(me, acc, mine, sent):
+def where():
+    member = lax.axis_index("group")
+    return lax.axis_index("space"), member & 1, member >> 1 & 1
+
+
+def write_halves(acc, mine, sent):
+    me = where()[0]
     rows = mine.shape[0]
     mine[...] = acc[pl.ds(pl.multiple_of((me & 1) * rows, rows), rows), :]
     sent[...] = acc[pl.ds(pl.multiple_of((1 - (me & 1)) * rows, rows), rows), :]
@@ -125,7 +130,7 @@
     return call(divide_kernel, 4, [VMEM], outs, [], x)
 
 
-def own_gram_kernel(ids, *refs):
+def own_gram_kernel(*refs):
     blocks, (mine, sent, acc) = refs[:-3], refs[-3:]
     total = None
     for block in blocks:
@@ -134,19 +139,16 @@
             part = dot_t(x, x)
             total = part if total is None else total + part
     acc[...] = total
-    write_halves(ids[0], acc, mine, sent)
-
-
-def own_gram(ids, blocks):
+    write_halves(acc, mine, sent)
+
+
+def own_gram(blocks):
     width = blocks[0].shape[-1]
     scratch = [pltpu.VMEM((width, width), F32)]
-    return call(
-        own_gram_kernel, 12, [SMEM] + [VMEM] * len(blocks), halves(width), scratch,
-        ids, *blocks,
-    )
-
-
-def cross_kernel(begin, chained, last, ids, own, other, *refs):
+    return call(own_gram_kernel, 12, [VMEM] * len(blocks), halves(width), scratch, *blocks)
+
+
+def cross_kernel(begin, level, chained, last, own, other, *refs):
     if chained:
         start, refs = refs[0], refs[1:]
     outs, acc = refs[:-1], refs[-1]
@@ -160,43 +162,44 @@
             total = part if total is None else total + part
         acc[...] = total
 
-    pl.when(ids[1] == 0)(lambda: add(0))
-    pl.when(ids[1] == 1)(lambda: add(1))
+    bit = lax.axis_index("group") >> level & 1
+    pl.when(bit == 0)(lambda: add(0))
+    pl.when(bit == 1)(lambda: add(1))
     if last:
-        write_halves(ids[0], acc, *outs)
+        write_halves(acc, *outs)
     else:
         outs[0][...] = acc[...]
 
 
-def cross_gram(ids, own, other, begin, start, last):
+def cross_gram(own, other, begin, level, start, last):
     width = own.shape[-1]
     chained = start is not None
     outs = halves(width) if last else [shape((width, width), F32)]
     return call(
-        functools.partial(cross_kernel, begin, chained, last),
-        8, [SMEM] + [VMEM] * (2 + chained), outs,
+        functools.partial(cross_kernel, begin, level, chained, last),
+        8, [VMEM] * (2 + chained), outs,
         [pltpu.VMEM((width, width), F32)],
-        ids, own, other, *([start] if chained else []),
-    )
-
-
-def share_kernel(ids, mine, got, *refs):
+        own, other, *([start] if chained else []),
+    )
+
+
+def share_kernel(mine, got, *refs):
     outs, acc = refs[:-1], refs[-1]
     acc[...] = mine[...] + got[...]
     rows = outs[0].shape[0]
     for k, out in enumerate(outs):
-        start = pl.multiple_of(jnp.bitwise_xor(ids[0] >> 1, k) * rows, rows)
+        start = pl.multiple_of(jnp.bitwise_xor(where()[0] >> 1, k) * rows, rows)
         out[...] = acc[pl.ds(start, rows), :]
 
 
-def scatter_space(ids, mine, sent):
+def scatter_space(mine, sent):
     chips = lax.axis_size("space") // 2
     rows, width = mine.shape
     got = swap(sent, "space", 1)
     slices = call(
-        share_kernel, 4, [SMEM, VMEM, VMEM],
+        share_kernel, 4, [VMEM, VMEM],
         [shape((rows // chips, width), F32)] * chips, [pltpu.VMEM((rows, width), F32)],
-        ids, mine, got,
+        mine, got,
     )
     total = slices[0]
     got = [swap(slices[k], "space", 2 * k) for k in range(1, chips)]
@@ -215,29 +218,29 @@
     return pieces
 
 
-def assemble_kernel(ids, *refs):
+def assemble_kernel(*refs):
     pieces, out = refs[:-1], refs[-1]
     rows, width = pieces[0].shape[1:]
     for k, piece in enumerate(pieces):
-        out[:, pl.ds(place(ids[0], k, rows, width), rows), :] = piece[...]
-
-
-def assemble(ids, pieces):
+        out[:, pl.ds(place(k, rows, width), rows), :] = piece[...]
+
+
+def assemble(pieces):
     lead, rows, width = pieces[0].shape
     return call(
-        assemble_kernel, 4, [SMEM] + [VMEM] * len(pieces),
-        [shape((lead, rows * len(pieces), width), F32)], [], ids, *pieces,
+        assemble_kernel, 4, [VMEM] * len(pieces),
+        [shape((lead, rows * len(pieces), width), F32)], [], *pieces,
     )[0]
 
 
-def run_filter(pairs, ids, diag, given, pieces, gram, iterate):
+def run_filter(pairs, diag, given, pieces, gram, iterate):
     rows, width = pieces[0].shape[1:]
     full = 2 * width
     for p in range(pairs):
         gram[p, :width, :width] = diag[2 * p]
         gram[p, width:, width:] = diag[2 * p + 1]
         for k, piece in enumerate(pieces):
-            gram[p, pl.ds(place(ids[0], k, rows, width), rows), width:] = piece[p]
+            gram[p, pl.ds(place(k, rows, width), rows), width:] = piece[p]
         gram[p, width:, :width] = gram[p, :width, width:].T
     eye = lax.broadcasted_iota(jnp.int32, (full, full), 0) == lax.broadcasted_iota(
         jnp.int32, (full, full), 1
@@ -270,20 +273,20 @@
     return mixes
 
 
-def pair_filter_kernel(ids, diag, sketch, *refs):
+def pair_filter_kernel(diag, sketch, *refs):
     pieces, (mix_ref, gram, iterate) = refs[:-3], refs[-3:]
-    mixes = run_filter(2, ids, diag, sketch[0], pieces, gram, iterate)
+    mixes = run_filter(2, diag, sketch[0], pieces, gram, iterate)
     for p in range(2):
         mix_ref[p] = mixes[p].reshape(mix_ref.shape[1:])
 
 
-def pair_filter(ids, diag, pieces, sketch):
+def pair_filter(diag, pieces, sketch):
     pairs, _, width = pieces[0].shape
     outs = [shape((pairs, 2, width, width), BF16), shape((pairs, 2 * width, 2 * width), F32)]
     return call(
-        pair_filter_kernel, 20, [SMEM] + [VMEM] * (2 + len(pieces)), outs,
+        pair_filter_kernel, 20, [VMEM] * (2 + len(pieces)), outs,
         [pltpu.VMEM((pairs, 2 * width, 2 * width), F32)],
-        ids, diag, sketch, *pieces,
+        diag, sketch, *pieces,
     )
 
 
@@ -310,8 +313,8 @@
         begin -= piece.shape[1]
 
 
-def merge_own_kernel(ids, mix, mine, near_head, near_tail, out):
-    bit0, bit1 = ids[1], ids[2]
+def merge_own_kernel(mix, mine, near_head, near_tail, out):
+    _, bit0, bit1 = where()
     tile = math.gcd(512, near_head.shape[1], near_tail.shape[1])
     for h in range(mine.shape[0]):
         for b in range(0, mine.shape[1], tile):
@@ -320,20 +323,20 @@
             out[h, b : b + tile, :] = total.astype(BF16)
 
 
-def merge_own(ids, mix, mine, *near):
-    return call(
-        merge_own_kernel, 8, [SMEM] + [VMEM] * 4, [shape(mine.shape, BF16)], [],
-        ids, mix, mine, *near,
+def merge_own(mix, mine, *near):
+    return call(
+        merge_own_kernel, 8, [VMEM] * 4, [shape(mine.shape, BF16)], [],
+        mix, mine, *near,
     )[0]
 
 
-def merge_other_kernel(begin, segments, chained, ids, mix, own, keep, risen, *refs):
+def merge_other_kernel(begin, segments, chained, mix, own, keep, risen, *refs):
     count = len(segments)
     left, passed, refs = refs[:count], refs[count : 2 * count], refs[2 * count :]
     if chained:
         start, refs = refs[0], refs[1:]
     out, *outs, acc = refs
-    bit0, bit1 = ids[1], ids[2]
+    _, bit0, bit1 = where()
     pair = 1 - bit1
     acc[...] = start[...] if chained else jnp.zeros(acc.shape, F32)
     outer, total_rows, _ = out.shape
@@ -350,7 +353,7 @@
     def near():
         merge(
             lambda k, h, skip, rows, at: left[k][h, skip : skip + rows, :],
-            lambda k, h, skip, rows, at: keep[h, begin + at : begin + at + rows, :],
+            lambda k, h, skip, rows, at: keep[h, at : at + rows, :],
         )
 
     def distant():
@@ -370,53 +373,65 @@
     pl.when(bit1 == 0)(lambda: add(0))
     pl.when(bit1 == 1)(lambda: add(1))
     if chained:
-        write_halves(ids[0], acc, *outs)
+        write_halves(acc, *outs)
     else:
         outs[0][...] = acc[...]
 
 
-def merge_other(begin, segments, start, ids, mix, own, keep, risen, left, passed):
+def merge_other(begin, segments, start, mix, own, keep, risen, left, passed):
     outer, _, width = own.shape
     chained = start is not None
     outs = halves(width) if chained else [shape((width, width), F32)]
-    args = [ids, mix, own, keep, risen, *left, *passed] + ([start] if chained else [])
+    args = [mix, own, keep, risen, *left, *passed] + ([start] if chained else [])
     rows = sum(size for _, size in segments)
     return call(
         functools.partial(merge_other_kernel, begin, segments, chained), 12,
-        [SMEM] + [VMEM] * (len(args) - 1), [shape((outer, rows, width), BF16)] + outs,
+        [VMEM] * len(args), [shape((outer, rows, width), BF16)] + outs,
         [pltpu.VMEM((width, width), F32)], *args,
     )
 
 
-def merge_filter_kernel(which, level, last, cuts, ids, diag, sketch, own, *refs):
+def merge_filter_kernel(level, last, cuts, diag, sketch, own, *refs):
     others, refs = refs[:cuts], refs[cuts:]
-    count = 3 if last else 4
-    pieces, refs = refs[:-count], refs[-count:]
-    out, mix_ref, gram, iterate = refs[0], refs[-2 if last else 1], None, refs[-1]
-    if last:
-        gram = refs[-2]
-        mix_ref = None
-    else:
-        gram = refs[2]
-    mix = run_filter(1, ids, diag, sketch[level], pieces, gram, iterate)[0]
+    count = 5 if last else 6
+    pieces, (out, *refs, stage, sems) = refs[:-count], refs[-count:]
+    gram, iterate = refs[-2:]
+    mix = run_filter(1, diag, sketch[level], pieces, gram, iterate)[0]
     width = diag.shape[-1]
-    bit = ids[which]
-
-    def finish(low, high):
+    bit = lax.axis_index("group") >> level & 1
+    tiles = []
+    for other in others:
+        begin = tiles[-1][2] + tiles[-1][3] if tiles else 0
+        size = math.gcd(512, other.shape[1]) if other.shape[1] <= 512 else other.shape[1] // 2
+        for skip in range(0, other.shape[1], size):
+            tiles.append((other, skip, begin + skip, size))
+    copies = []
+    for _, _, begin, size in tiles:
         for h in range(own.shape[0]):
-            for b in range(0, own.shape[1], tile):
-                total = dot(read(low, h, b, tile), mix[:width])
-                total += dot(read(high, h, b, tile), mix[width:])
-                out[h, b : b + tile, :] = total.astype(BF16)
-
-    tile = math.gcd(256, *(other.shape[1] for other in others))
-    pl.when(bit == 0)(lambda: finish([own], others))
-    pl.when(bit == 1)(lambda: finish(others, [own]))
+            here = pl.ds(begin, size)
+            copies.append(
+                pltpu.make_async_copy(
+                    stage.at[h, here, :], out.at[h, here, :], sems.at[len(copies)]
+                )
+            )
+
+    def finish(own_mix, other_mix):
+        for k, (other, skip, begin, size) in enumerate(tiles):
+            for h in range(own.shape[0]):
+                total = dot(own[h, begin : begin + size, :], own_mix)
+                total += dot(other[h, skip : skip + size, :], other_mix)
+                stage[h, begin : begin + size, :] = total.astype(BF16)
+                copies[k * own.shape[0] + h].start()
+
+    pl.when(bit == 0)(lambda: finish(mix[:width], mix[width:]))
+    pl.when(bit == 1)(lambda: finish(mix[width:], mix[:width]))
     if not last:
-        mix_ref[0] = mix.reshape(mix_ref.shape[1:])
-
-
-def merge_filter(ids, which, level, last, diag, pieces, sketch, own, others):
+        refs[0][0] = mix.reshape(refs[0].shape[1:])
+    for copy in copies:
+        copy.wait()
+
+
+def merge_filter(level, last, diag, pieces, sketch, own, others):
     width = diag.shape[-1]
     square = (1, 2 * width, 2 * width)
     outs = [shape(own.shape, BF16)]
@@ -424,11 +439,17 @@
     if not last:
         outs += [shape((1, 2, width, width), BF16), shape(square, F32)]
         scratch = scratch[:1]
-    return call(
-        functools.partial(merge_filter_kernel, which, level, last, len(others)),
-        20, [SMEM] + [VMEM] * (3 + len(others) + len(pieces)), outs, scratch,
-        ids, diag, sketch, own, *others, *pieces,
-    )
+    count = own.shape[0] * 4 * len(others)
+    scratch += [pltpu.VMEM(own.shape, BF16), pltpu.SemaphoreType.DMA((count,))]
+    return pl.pallas_call(
+        functools.partial(merge_filter_kernel, level, last, len(others)),
+        in_specs=[VMEM] * (3 + len(others) + len(pieces)),
+        out_specs=[HBM] + [VMEM] * (len(outs) - 1),
+        out_shape=outs,
+        scratch_shapes=scratch,
+        compiler_params=pltpu.CompilerParams(vmem_limit_bytes=20 * 2**20),
+        name="merge_filter",
+    )(diag, sketch, own, *others, *pieces)
 
 
 def compute(snapshot_basis, sketch):
@@ -436,13 +457,11 @@
     groups = lax.axis_size("group")
     levels = groups.bit_length() - 1
     member = lax.axis_index("group")
-    bit0 = member & 1
     bit1 = member >> 1 & 1
-    ids = jnp.stack([lax.axis_index("space"), bit0, bit1]).astype(jnp.int32)
     block_rows = rows // groups
     cut = block_rows * 3 // 4
     tail = block_rows - cut
-    part = block_rows * 7 // 16
+    part = block_rows * 3 // 8
 
     middle, forward, rise, leave = [], [], [], []
     for base in range(0, groups, 4):
@@ -459,8 +478,8 @@
             (1, 0, cut, tail)]
     near_own, tail_own, mine, leave_head, leave_tail = pick(after(snapshot_basis, far_own), 48, cuts)
 
-    own_halves = own_gram(ids, [far_own, across, near_own, tail_own, mine])
-    own_sum = scatter_space(ids, *own_halves)
+    own_halves = own_gram([far_own, across, near_own, tail_own, mine])
+    own_sum = scatter_space(*own_halves)
     turned = [own_sum] + [swap(own_sum, "group", k) for k in (1, 2, 3)]
 
     near_head = send(after(near_own, own_sum), pair)
@@ -474,12 +493,12 @@
     diag_slices = jnp.stack(
         [lax.dynamic_index_in_dim(stacked, quad ^ g, 0, keepdims=False) for g in range(4)]
     )
-    diag = assemble(ids, gather_space(diag_slices))
-
-    cross = cross_gram(ids, across, far, 0, None, False)[0]
-    cross = cross_gram(ids, mine, near_head, 0, cross, False)[0]
-    cross_halves = cross_gram(ids, mine, near_tail, cut, cross, True)
-    cross_sum = scatter_space(ids, *cross_halves)
+    diag = assemble(gather_space(diag_slices))
+
+    cross = cross_gram(across, far, 0, 0, None, False)[0]
+    cross = cross_gram(mine, near_head, 0, 0, cross, False)[0]
+    cross_halves = cross_gram(mine, near_tail, cut, 0, cross, True)
+    cross_sum = scatter_space(*cross_halves)
     one, two, three = [swap(cross_sum, "group", k) for k in (1, 2, 3)]
     here = cross_sum + one
     there = two + three
@@ -492,22 +511,23 @@
     left_tail = send(after(leave_tail, cross_sum), leave)
     pass_tail = send(after(pass_parts[1], cross_sum), forward)
 
-    mix, gram = pair_filter(ids, diag, gather_space(both), sketch)
+    mix, gram = pair_filter(diag, gather_space(both), sketch)
     diag = next_diag(gram, mix)
-    own_merged = merge_own(ids, mix, mine, near_head, near_tail)
-    args = [ids, mix, own_merged, keep]
+    own_merged = merge_own(mix, mine, near_head, near_tail)
+    args = [mix, own_merged]
+    keep_head, keep_tail = divide(keep, part)
     other_head, cross = merge_other(
-        0, [(0, part)], None, *args, rise_head, [left_head], [pass_head]
+        0, [(0, part)], None, *args, keep_head, rise_head, [left_head], [pass_head]
     )
     other_tail, *both_halves = merge_other(
-        part, [(part, cut - part), (0, tail)], cross, *args, rise_tail,
+        part, [(part, cut - part), (0, tail)], cross, *args, keep_tail, rise_tail,
         [left_head, left_tail], [pass_head, pass_tail],
     )
-    total = scatter_space(ids, *both_halves)
+    total = scatter_space(*both_halves)
     one, two, three = [swap(total, "group", k) for k in (1, 2, 3)]
     total = (total + one) + (two + three)
     result = merge_filter(
-        ids, 2, 1, levels == 2, diag, gather_space(total[None]), sketch,
+        1, levels == 2, diag, gather_space(total[None]), sketch,
         own_merged, [other_head, other_tail],
     )
 
@@ -520,15 +540,14 @@
         got = swap(given, "group", 1 << level)
         diag_own = next_diag(result[2], result[1])[0]
         diag_got = swap(diag_own, "group", 1 << level)
-        flags = jnp.stack([lax.axis_index("space"), bit]).astype(jnp.int32)
-        total = scatter_space(flags, *cross_gram(flags, kept, got, 0, None, True))
+        total = scatter_space(*cross_gram(kept, got, 0, level, None, True))
         for low in range(level + 1):
             total = total + swap(total, "group", 1 << low)
         diag = jnp.stack(
             [jnp.where(bit == 0, diag_own, diag_got), jnp.where(bit == 0, diag_got, diag_own)]
         )
         result = merge_filter(
-            flags, 1, level, level + 1 == levels, diag, gather_space(total[None]),
+            level, level + 1 == levels, diag, gather_space(total[None]),
             sketch, kept, [got],
         )
     return result[0].reshape(block_rows, width)

time: 186 us -> 186 us (level)
  waiting for transfers between devices: 72.7 us -> 82.3 us
  Pallas kernels: 42.4 us -> 35.4 us
  local copies, waits for them, and re-layouts: 6.3 us -> 3.43 us
    ppermute x11, waiting for transfers between devices: 11.2 us -> 49.2 us  [send(): return lax.ppermute(value, 'group', routes)]
    ppermute x42, waiting for transfers between devices: 61.4 us -> 33.1 us  [swap(): return lax.ppermute(block, axis, [(i, i ^ offset) for i in range(count)])]
    pallas_call x18, Pallas kernels: 42.4 us -> 27.6 us  [call(): pl.pallas_call(kernel, in_specs=in_specs, out_specs=[VMEM] * len(outs), o...]
    pallas_call x0 -> x1, Pallas kernels: none -> 7.85 us  [merge_filter(): pl.pallas_call(functools.partial(merge_filter_kernel, level, last, len(ot...]
    unnamed x22 -> x18, local copies, waits for them, and re-layouts: 6.27 us -> 3.41 us
  transfers between devices with their start and end apart: 53 -> 53, of which waited for: 26 -> 28; matrix products, arithmetic and copies ran while one was open for 1% -> 1% of each run, Pallas kernels for 12% -> 10%
where the time goes in v2:
time: 186 us
  waiting for transfers between devices  82.3 us (44%)
  starting transfers between devices  62.6 us (34%)
  Pallas kernels  35.4 us (19%)
  local copies, waits for them, and re-layouts  3.43 us (2%)
    ppermute x11, waiting for transfers between devices, send(): return lax.ppermute(value, 'group', routes)  49.2 us
    ppermute x42, starting transfers between devices, swap(): return lax.ppermute(block, axis, [(i, i ^ offset) for i in range(count)])  38.9 us
    ppermute x42, waiting for transfers between devices, swap(): return lax.ppermute(block, axis, [(i, i ^ offset) for i in range(count)])  33.1 us
    pallas_call x18, Pallas kernels, call(): pl.pallas_call(kernel, in_specs=in_specs, out_specs=[VMEM] * len(outs), o...  27.6 us
    ppermute x11, starting transfers between devices, send(): return lax.ppermute(value, 'group', routes)  23.7 us
    pallas_call x1, Pallas kernels, merge_filter(): pl.pallas_call(functools.partial(merge_filter_kernel, level, last, len(ot...  7.85 us
  transfers between devices with their start and end apart: 53, of which 28 were waited for; matrix products, arithmetic and copies ran while one was open for 1% of the time, Pallas kernels for 10%

profile of v2, /device:TPU:0, one launch (start us, length us, event | category | flops | bytes accessed | tf_op | source)
XLA Modules:
  0.0 185.9 jit_solution(5085712806396921778)
XLA Ops:
  0.0 2.9 %shard_map.28 = (bf16[1,2048,256]{2,1,0:T(8,128)(2,1)}, bf16[1,2048,256]{2,1,0:T(8,128)(2,1)}) custom-call(bf16[8192,256]{1,0:T(8,128)(2,1)} %x_ref.2), custom_call_target="tpu_custom_call" | custom-call | tf_op jit(solution)/shard_map/pallas_call | solution.py:56
  2.9 1.9 %shard_map.29 = (bf16[1,1536,256]{2,1,0:T(8,128)(2,1)S(1)}, bf16[1,512,256]{2,1,0:T(8,128)(2,1)S(1)}, bf16[1,2048,256]{2,1,0:T(8,128)(2,1)S(1)}, bf16[1,1536,256...) custom-call(bf16[8192,256]{1,0:T(8,128)(2,1)} %x_ref.2), custom_call_target="tpu_custom_call" | custom-call | tf_op jit(solution)/shard_map/pallas_call | solution.py:56
  6.4 2.9 %shard_map.30 = (f32[128,256]{1,0:T(8,128)S(1)}, f32[128,256]{1,0:T(8,128)S(1)}) custom-call(bf16[1,2048,256]{2,1,0:T(8,128)(2,1)} %get-tuple-element.73.refs_0_, bf16[1,2048,256]{2,1,0:T(8,128)(2,1)} %get-tuple-element.52.refs_1_.own, bf16[1,1536,256]{2,1,0:T(8,128)(2,1)S(1)} %get-tuple-element.64.refs_2_, ...), custom_call_target="tpu_custom_call" | custom-call | tf_op jit(solution)/shard_map/pallas_call | solution.py:56
  10.8 2.9 %collective-permute-start.1 = (f32[32,256]{1,0:T(8,128)S(1)}, f32[32,256]{1,0:T(8,128)S(1)}, u32[]{:S(2)}, u32[]{:S(2)}) collective-permute-start(f32[32,256]{1,0:T(8,128)S(1)} %get-tuple-element.60), channel_id=1, source_target_pairs={{0,8},{4,12},{8,0},{12,4},{16,24},{20,28},{24,16},{28,20},{1,9},{5... | collective-permute-start | bytes 98312 | tf_op jit(solution)/shard_map/ppermute | solution.py:21
  15.3 2.0 %collective-permute-start.16 = (bf16[1,2048,256]{2,1,0:T(8,128)(2,1)}, bf16[1,2048,256]{2,1,0:T(8,128)(2,1)S(1)}, u32[]{:S(2)}, u32[]{:S(2)}) collective-permute-start(bf16[1,2048,256]{2,1,0:T(8,128)(2,1)} %get-tuple-element.73.refs_0_), channel_id=1, source_target_pairs={{0,1},{1,0},{2,3},{3,2},{4,5},{5,4},{6,7},{7,6},{8,9},{9,8},{10,11... | collective-permute-start | bytes 3145736 | tf_op jit(solution)/shard_map/ppermute | solution.py:25
  17.6 2.4 %collective-permute-done.3 = f32[32,256]{1,0:T(8,128)S(1)} collective-permute-done((f32[32,256]{1,0:T(8,128)S(1)}, f32[32,256]{1,0:T(8,128)S(1)}, u32[]{:S(2)}, u32[]{:S(2)}) %collective-permute-start.3) | collective-permute-done | bytes 32800 | tf_op jit(solution)/shard_map/ppermute | solution.py:21
  23.4 3.5 %collective-permute-start.14 = (bf16[1,512,256]{2,1,0:T(8,128)(2,1)S(1)}, bf16[1,512,256]{2,1,0:T(8,128)(2,1)S(1)}, u32[]{:S(2)}, u32[]{:S(2)}) collective-permute-start(bf16[1,512,256]{2,1,0:T(8,128)(2,1)S(1)} %get-tuple-element.63.refs_3_), channel_id=1, source_target_pairs={{0,1},{1,0},{2,3},{3,2},{4,5},{5,4},{6,7},{7,6},{8,9},{9,8},{10,11... | collective-permute-start | bytes 786440 | tf_op jit(solution)/shard_map/ppermute | solution.py:25
  27.7 34.9 %collective-permute-done.14.other.near_tail = bf16[1,512,256]{2,1,0:T(8,128)(2,1)S(1)} collective-permute-done((bf16[1,512,256]{2,1,0:T(8,128)(2,1)S(1)}, bf16[1,512,256]{2,1,0:T(8,128)(2,1)S(1)}, u32[]{:S(2)}, u32[]{:S(2)}) %collective-permute-start.14) | collective-permute-done | bytes 262176 | tf_op jit(solution)/shard_map/ppermute | solution.py:25
  62.6 3.1 %collective-permute-start.5 = (f32[32,256]{1,0:T(8,128)S(1)}, f32[32,256]{1,0:T(8,128)S(1)}, u32[]{:S(2)}, u32[]{:S(2)}) collective-permute-start(f32[32,256]{1,0:T(8,128)S(1)} %add_add_fusion.2), channel_id=1, source_target_pairs={{0,2},{1,3},{2,0},{3,1},{4,6},{5,7},{6,4},{7,5},{8,10},{9,11},{10,... | collective-permute-start | bytes 98312 | tf_op jit(solution)/shard_map/ppermute | solution.py:21
  65.7 1.9 %collective-permute-start.4 = (f32[32,256]{1,0:T(8,128)S(1)}, f32[32,256]{1,0:T(8,128)S(1)}, u32[]{:S(2)}, u32[]{:S(2)}) collective-permute-start(f32[32,256]{1,0:T(8,128)S(1)} %add_add_fusion.2), channel_id=1, source_target_pairs={{0,1},{1,0},{2,3},{3,2},{4,5},{5,4},{6,7},{7,6},{8,9},{9,8},{10,11... | collective-permute-start | bytes 98312 | tf_op jit(solution)/shard_map/ppermute | solution.py:21
  77.3 2.5 %collective-permute-start.12 = (f32[4,32,256]{2,1,0:T(8,128)S(1)}, f32[4,32,256]{2,1,0:T(8,128)S(1)}, u32[]{:S(2)}, u32[]{:S(2)}) collective-permute-start(f32[4,32,256]{2,1,0:T(8,128)S(1)} %pad_maximum_fusion.1.refs_0_), channel_id=1, source_target_pairs={{0,24},{4,28},{8,16},{12,20},{16,8},{20,12},{24,0},{28,4},{1,25},{... | collective-permute-start | bytes 393224 | tf_op jit(solution)/shard_map/ppermute | solution.py:21
  85.8 2.2 %collective-permute-start.22 = (f32[32,256]{1,0:T(8,128)}, f32[32,256]{1,0:T(8,128)}, u32[]{:S(2)}, u32[]{:S(2)}) collective-permute-start(f32[32,256]{1,0:T(8,128)} %add_add_fusion.1), channel_id=1, source_target_pairs={{0,2},{1,3},{2,0},{3,1},{4,6},{5,7},{6,4},{7,5},{8,10},{9,11},{10,... | collective-permute-start | bytes 98312 | tf_op jit(solution)/shard_map/ppermute | solution.py:21
  90.4 4.4 %collective-permute-done.22 = f32[32,256]{1,0:T(8,128)} collective-permute-done((f32[32,256]{1,0:T(8,128)}, f32[32,256]{1,0:T(8,128)}, u32[]{:S(2)}, u32[]{:S(2)}) %collective-permute-start.22) | collective-permute-done | bytes 32800 | tf_op jit(solution)/shard_map/ppermute | solution.py:21
  96.2 3.0 %collective-permute-start.33 = (bf16[1,1536,256]{2,1,0:T(8,128)(2,1)}, bf16[1,1536,256]{2,1,0:T(8,128)(2,1)S(1)}, u32[]{:S(2)}, u32[]{:S(2)}) collective-permute-start(bf16[1,1536,256]{2,1,0:T(8,128)(2,1)} %copy-done.7), channel_id=1, source_target_pairs={{0,2},{3,1},{4,6},{7,5},{8,10},{11,9},{12,14},{15,13},{16,18},{19,... | collective-permute-start | bytes 2359304 | tf_op jit(solution)/shard_map/ppermute | solution.py:25
  100.5 2.5 %collective-permute-start.29 = (f32[2,32,256]{2,1,0:T(8,128)S(1)}, f32[2,32,256]{2,1,0:T(8,128)S(1)}, u32[]{:S(2)}, u32[]{:S(2)}) collective-permute-start(f32[2,32,256]{2,1,0:T(8,128)S(1)} %pad_maximum_fusion.2.refs_0_), channel_id=1, source_target_pairs={{0,24},{4,28},{8,16},{12,20},{16,8},{20,12},{24,0},{28,4},{1,25},{... | collective-permute-start | bytes 196616 | tf_op jit(solution)/shard_map/ppermute | solution.py:21
  108.6 3.1 %collective-permute-done.25.refs_2_ = f32[2,32,256]{2,1,0:T(8,128)S(1)} collective-permute-done((f32[2,32,256]{2,1,0:T(8,128)S(1)}, f32[2,32,256]{2,1,0:T(8,128)S(1)}, u32[]{:S(2)}, u32[]{:S(2)}) %collective-permute-start.25) | collective-permute-done | bytes 65568 | tf_op jit(solution)/shard_map/ppermute | solution.py:21
  116.8 5.2 %collective-permute-start.37 = (bf16[1,512,256]{2,1,0:T(8,128)(2,1)}, bf16[1,512,256]{2,1,0:T(8,128)(2,1)S(1)}, u32[]{:S(2)}, u32[]{:S(2)}) collective-permute-start(bf16[1,512,256]{2,1,0:T(8,128)(2,1)} %copy-done.8), channel_id=1, source_target_pairs={{0,2},{3,1},{4,6},{7,5},{8,10},{11,9},{12,14},{15,13},{16,18},{19,... | collective-permute-start | bytes 786440 | tf_op jit(solution)/shard_map/ppermute | solution.py:25
  121.9 11.1 %collective-permute-done.32.risen = bf16[1,768,256]{2,1,0:T(8,128)(2,1)S(1)} collective-permute-done((bf16[1,768,256]{2,1,0:T(8,128)(2,1)S(1)}, bf16[1,768,256]{2,1,0:T(8,128)(2,1)S(1)}, u32[]{:S(2)}, u32[]{:S(2)}) %collective-permute-start.32) | collective-permute-done | bytes 393248 | tf_op jit(solution)/shard_map/ppermute | solution.py:25
  138.4 9.2 %shard_map.37 = (bf16[2,2,256,256]{3,2,1,0:T(8,128)(2,1)S(1)}, f32[2,512,512]{2,1,0:T(8,128)S(1)}) custom-call(f32[4,256,256]{2,1,0:T(8,128)S(1)} %shard_map.32.diag, f32[2,512,256]{2,1,0:T(8,128)S(1)} %copy-done, f32[2,32,256]{2,1,0:T(8,128)S(1)} %pad_maximum_fusion.2.refs_0_, f32[2,32,256]{2,1,0:T(8,128)S(1)} %collective-permute-done.24.refs_1_, ...), custom_call_target="tpu_custom_call" | custom-call | tf_op jit(solution)/shard_map/pallas_call | solution.py:56
  149.4 3.2 %collective-permute-done.38.refs_3_ = bf16[1,512,256]{2,1,0:T(8,128)(2,1)S(1)} collective-permute-done((bf16[1,512,256]{2,1,0:T(8,128)(2,1)S(1)}, bf16[1,512,256]{2,1,0:T(8,128)(2,1)S(1)}, u32[]{:S(2)}, u32[]{:S(2)}) %collective-permute-start.38) | collective-permute-done | bytes 262176 | tf_op jit(solution)/shard_map/ppermute | solution.py:25
  160.4 2.4 %collective-permute-done.42 = f32[32,256]{1,0:T(8,128)S(1)} collective-permute-done((f32[32,256]{1,0:T(8,128)S(1)}, f32[32,256]{1,0:T(8,128)S(1)}, u32[]{:S(2)}, u32[]{:S(2)}) %collective-permute-start.42) | collective-permute-done | bytes 32800 | tf_op jit(solution)/shard_map/ppermute | solution.py:21
  162.9 2.3 %collective-permute-start.45 = (f32[32,256]{1,0:T(8,128)S(1)}, f32[32,256]{1,0:T(8,128)S(1)}, u32[]{:S(2)}, u32[]{:S(2)}) collective-permute-start(f32[32,256]{1,0:T(8,128)S(1)} %add_add_fusion), channel_id=1, source_target_pairs={{0,3},{1,2},{2,1},{3,0},{4,7},{5,6},{6,5},{7,4},{8,11},{9,10},{10,... | collective-permute-start | bytes 98312 | tf_op jit(solution)/shard_map/ppermute | solution.py:21
  165.2 2.2 %collective-permute-start.43 = (f32[32,256]{1,0:T(8,128)S(1)}, f32[32,256]{1,0:T(8,128)S(1)}, u32[]{:S(2)}, u32[]{:S(2)}) collective-permute-start(f32[32,256]{1,0:T(8,128)S(1)} %add_add_fusion), channel_id=1, source_target_pairs={{0,1},{1,0},{2,3},{3,2},{4,5},{5,4},{6,7},{7,6},{8,9},{9,8},{10,11... | collective-permute-start | bytes 98312 | tf_op jit(solution)/shard_map/ppermute | solution.py:21
  177.9 7.8 %merge_filter.1 = bf16[1,2048,256]{2,1,0:T(8,128)(2,1)} custom-call(f32[2,256,256]{2,1,0:T(8,128)S(1)} %shard_map.38.diag, f32[2,512,256]{2,1,0:T(8,128)S(1)} %copy-done, bf16[1,2048,256]{2,1,0:T(8,128)(2,1)S(1)} %shard_map.39.own, bf16[1,768,256]{2,1,0:T(8,128)(2,1)S(1)} %get-tuple-element.81.refs_0_, bf16[1,1280,256]{2,1,0:T(8,128)(2,1)S(1)} %get-tuple-element.90.refs_1_, ...), custom_call_target="tpu_custom_call" | custom-call | tf_op jit(solution)/shard_map/merge_filter/pallas_call | solution.py:444
  (128 shorter events, 65.8 us)
Async XLA Ops:
  10.8 6.5 %collective-permute-start.1 = (f32[32,256]{1,0:T(8,128)S(1)}, f32[32,256]{1,0:T(8,128)S(1)}, u32[]{:S(2)}, u32[]{:S(2)}) collective-permute-start(f32[32,256]{1,0:T(8,128)S(1)} %get-tuple-element.60), channel_id=1, source_target_pairs={{0,8},{4,12},{8,0},{12,4},{16,24},{20,28},{24,16},{28,20},{1,9},{5... | collective-permute-start | bytes 98312 | tf_op jit(solution)/shard_map/ppermute | solution.py:21
  15.3 52.4 %collective-permute-start.16 = (bf16[1,2048,256]{2,1,0:T(8,128)(2,1)}, bf16[1,2048,256]{2,1,0:T(8,128)(2,1)S(1)}, u32[]{:S(2)}, u32[]{:S(2)}) collective-permute-start(bf16[1,2048,256]{2,1,0:T(8,128)(2,1)} %get-tuple-element.73.refs_0_), channel_id=1, source_target_pairs={{0,1},{1,0},{2,3},{3,2},{4,5},{5,4},{6,7},{7,6},{8,9},{9,8},{10,11... | collective-permute-start | bytes 3145736 | tf_op jit(solution)/shard_map/ppermute | solution.py:25
  20.1 45.6 %collective-permute-start.15 = (bf16[1,1536,256]{2,1,0:T(8,128)(2,1)S(1)}, bf16[1,1536,256]{2,1,0:T(8,128)(2,1)S(1)}, u32[]{:S(2)}, u32[]{:S(2)}) collective-permute-start(bf16[1,1536,256]{2,1,0:T(8,128)(2,1)S(1)} %get-tuple-element.64.refs_2_), channel_id=1, source_target_pairs={{0,1},{1,0},{2,3},{3,2},{4,5},{5,4},{6,7},{7,6},{8,9},{9,8},{10,11... | collective-permute-start | bytes 2359304 | tf_op jit(solution)/shard_map/ppermute | solution.py:25
  21.7 66.3 %collective-permute-start.34 = (bf16[1,2048,256]{2,1,0:T(8,128)(2,1)}, bf16[1,2048,256]{2,1,0:T(8,128)(2,1)}, u32[]{:S(2)}, u32[]{:S(2)}) collective-permute-start(bf16[1,2048,256]{2,1,0:T(8,128)(2,1)} %get-tuple-element.52.refs_1_.own), channel_id=1, source_target_pairs={{1,2},{2,1},{5,6},{6,5},{9,10},{10,9},{13,14},{14,13},{17,18},{18,... | collective-permute-start | bytes 3145736 | tf_op jit(solution)/shard_map/ppermute | solution.py:25
  23.4 39.2 %collective-permute-start.14 = (bf16[1,512,256]{2,1,0:T(8,128)(2,1)S(1)}, bf16[1,512,256]{2,1,0:T(8,128)(2,1)S(1)}, u32[]{:S(2)}, u32[]{:S(2)}) collective-permute-start(bf16[1,512,256]{2,1,0:T(8,128)(2,1)S(1)} %get-tuple-element.63.refs_3_), channel_id=1, source_target_pairs={{0,1},{1,0},{2,3},{3,2},{4,5},{5,4},{6,7},{7,6},{8,9},{9,8},{10,11... | collective-permute-start | bytes 786440 | tf_op jit(solution)/shard_map/ppermute | solution.py:25
  26.8 45.0 %collective-permute-start.6 = (f32[32,256]{1,0:T(8,128)S(1)}, f32[32,256]{1,0:T(8,128)S(1)}, u32[]{:S(2)}, u32[]{:S(2)}) collective-permute-start(f32[32,256]{1,0:T(8,128)S(1)} %add_add_fusion.2), channel_id=1, source_target_pairs={{0,3},{1,2},{2,1},{3,0},{4,7},{5,6},{6,5},{7,4},{8,11},{9,10},{10,... | collective-permute-start | bytes 98312 | tf_op jit(solution)/shard_map/ppermute | solution.py:21
  62.6 9.3 %collective-permute-start.5 = (f32[32,256]{1,0:T(8,128)S(1)}, f32[32,256]{1,0:T(8,128)S(1)}, u32[]{:S(2)}, u32[]{:S(2)}) collective-permute-start(f32[32,256]{1,0:T(8,128)S(1)} %add_add_fusion.2), channel_id=1, source_target_pairs={{0,2},{1,3},{2,0},{3,1},{4,6},{5,7},{6,4},{7,5},{8,10},{9,11},{10,... | collective-permute-start | bytes 98312 | tf_op jit(solution)/shard_map/ppermute | solution.py:21
  65.7 6.2 %collective-permute-start.4 = (f32[32,256]{1,0:T(8,128)S(1)}, f32[32,256]{1,0:T(8,128)S(1)}, u32[]{:S(2)}, u32[]{:S(2)}) collective-permute-start(f32[32,256]{1,0:T(8,128)S(1)} %add_add_fusion.2), channel_id=1, source_target_pairs={{0,1},{1,0},{2,3},{3,2},{4,5},{5,4},{6,7},{7,6},{8,9},{9,8},{10,11... | collective-permute-start | bytes 98312 | tf_op jit(solution)/shard_map/ppermute | solution.py:21
  67.6 36.1 %collective-permute-start.31 = (bf16[1,2048,256]{2,1,0:T(8,128)(2,1)}, bf16[1,2048,256]{2,1,0:T(8,128)(2,1)}, u32[]{:S(2)}, u32[]{:S(2)}) collective-permute-start(bf16[1,2048,256]{2,1,0:T(8,128)(2,1)} %get-tuple-element.73.refs_0_), channel_id=1, source_target_pairs={{1,2},{2,1},{5,6},{6,5},{9,10},{10,9},{13,14},{14,13},{17,18},{18,... | collective-permute-start | bytes 3145736 | tf_op jit(solution)/shard_map/ppermute | solution.py:25
  77.3 6.7 %collective-permute-start.12 = (f32[4,32,256]{2,1,0:T(8,128)S(1)}, f32[4,32,256]{2,1,0:T(8,128)S(1)}, u32[]{:S(2)}, u32[]{:S(2)}) collective-permute-start(f32[4,32,256]{2,1,0:T(8,128)S(1)} %pad_maximum_fusion.1.refs_0_), channel_id=1, source_target_pairs={{0,24},{4,28},{8,16},{12,20},{16,8},{20,12},{24,0},{28,4},{1,25},{... | collective-permute-start | bytes 393224 | tf_op jit(solution)/shard_map/ppermute | solution.py:21
  79.7 6.0 %collective-permute-start.10 = (f32[4,32,256]{2,1,0:T(8,128)S(1)}, f32[4,32,256]{2,1,0:T(8,128)S(1)}, u32[]{:S(2)}, u32[]{:S(2)}) collective-permute-start(f32[4,32,256]{2,1,0:T(8,128)S(1)} %pad_maximum_fusion.1.refs_0_), channel_id=1, source_target_pairs={{0,16},{4,20},{8,24},{12,28},{16,0},{20,4},{24,8},{28,12},{1,17},{... | collective-permute-start | bytes 393224 | tf_op jit(solution)/shard_map/ppermute | solution.py:21
  81.6 8.3 %collective-permute-start.8 = (f32[4,32,256]{2,1,0:T(8,128)S(1)}, f32[4,32,256]{2,1,0:T(8,128)}, u32[]{:S(2)}, u32[]{:S(2)}) collective-permute-start(f32[4,32,256]{2,1,0:T(8,128)S(1)} %pad_maximum_fusion.1.refs_0_), channel_id=1, source_target_pairs={{0,8},{4,12},{8,0},{12,4},{16,24},{20,28},{24,16},{28,20},{1,9},{5... | collective-permute-start | bytes 393224 | tf_op jit(solution)/shard_map/ppermute | solution.py:21
  84.0 6.1 %collective-permute-start.23 = (f32[32,256]{1,0:T(8,128)}, f32[32,256]{1,0:T(8,128)}, u32[]{:S(2)}, u32[]{:S(2)}) collective-permute-start(f32[32,256]{1,0:T(8,128)} %add_add_fusion.1), channel_id=1, source_target_pairs={{0,3},{1,2},{2,1},{3,0},{4,7},{5,6},{6,5},{7,4},{8,11},{9,10},{10,... | collective-permute-start | bytes 98312 | tf_op jit(solution)/shard_map/ppermute | solution.py:21
  85.8 9.1 %collective-permute-start.22 = (f32[32,256]{1,0:T(8,128)}, f32[32,256]{1,0:T(8,128)}, u32[]{:S(2)}, u32[]{:S(2)}) collective-permute-start(f32[32,256]{1,0:T(8,128)} %add_add_fusion.1), channel_id=1, source_target_pairs={{0,2},{1,3},{2,0},{3,1},{4,6},{5,7},{6,4},{7,5},{8,10},{9,11},{10,... | collective-permute-start | bytes 98312 | tf_op jit(solution)/shard_map/ppermute | solution.py:21
  88.0 6.9 %collective-permute-start.21 = (f32[32,256]{1,0:T(8,128)}, f32[32,256]{1,0:T(8,128)}, u32[]{:S(2)}, u32[]{:S(2)}) collective-permute-start(f32[32,256]{1,0:T(8,128)} %add_add_fusion.1), channel_id=1, source_target_pairs={{0,1},{1,0},{2,3},{3,2},{4,5},{5,4},{6,7},{7,6},{8,9},{9,8},{10,11... | collective-permute-start | bytes 98312 | tf_op jit(solution)/shard_map/ppermute | solution.py:21
  89.9 6.4 %collective-permute-start.7 = (f32[4,32,256]{2,1,0:T(8,128)S(1)}, f32[4,32,256]{2,1,0:T(8,128)S(1)}, u32[]{:S(2)}, u32[]{:S(2)}) collective-permute-start(f32[4,32,256]{2,1,0:T(8,128)S(1)} %pad_maximum_fusion.1.refs_0_), channel_id=1, source_target_pairs={{0,4},{4,0},{8,12},{12,8},{16,20},{20,16},{24,28},{28,24},{1,5},{5... | collective-permute-start | bytes 393224 | tf_op jit(solution)/shard_map/ppermute | solution.py:21
  90.1 9.1 %collective-permute-start.13 = (f32[4,32,256]{2,1,0:T(8,128)}, f32[4,32,256]{2,1,0:T(8,128)S(1)}, u32[]{:S(2)}, u32[]{:S(2)}) collective-permute-start(f32[4,32,256]{2,1,0:T(8,128)} %copy-done.3), channel_id=1, source_target_pairs={{0,4},{4,0},{8,12},{12,8},{16,20},{20,16},{24,28},{28,24},{1,5},{5... | collective-permute-start | bytes 393224 | tf_op jit(solution)/shard_map/ppermute | solution.py:21
  94.9 8.3 %collective-permute-start.9 = (f32[4,32,256]{2,1,0:T(8,128)}, f32[4,32,256]{2,1,0:T(8,128)S(1)}, u32[]{:S(2)}, u32[]{:S(2)}) collective-permute-start(f32[4,32,256]{2,1,0:T(8,128)} %collective-permute-done.8.refs_2_), channel_id=1, source_target_pairs={{0,4},{4,0},{8,12},{12,8},{16,20},{20,16},{24,28},{28,24},{1,5},{5... | collective-permute-start | bytes 393224 | tf_op jit(solution)/shard_map/ppermute | solution.py:21
  96.2 52.2 %collective-permute-start.33 = (bf16[1,1536,256]{2,1,0:T(8,128)(2,1)}, bf16[1,1536,256]{2,1,0:T(8,128)(2,1)S(1)}, u32[]{:S(2)}, u32[]{:S(2)}) collective-permute-start(bf16[1,1536,256]{2,1,0:T(8,128)(2,1)} %copy-done.7), channel_id=1, source_target_pairs={{0,2},{3,1},{4,6},{7,5},{8,10},{11,9},{12,14},{15,13},{16,18},{19,... | collective-permute-start | bytes 2359304 | tf_op jit(solution)/shard_map/ppermute | solution.py:25
  99.2 49.2 %collective-permute-start.35 = (bf16[1,1536,256]{2,1,0:T(8,128)(2,1)S(1)}, bf16[1,1536,256]{2,1,0:T(8,128)(2,1)S(1)}, u32[]{:S(2)}, u32[]{:S(2)}) collective-permute-start(bf16[1,1536,256]{2,1,0:T(8,128)(2,1)S(1)} %get-tuple-element.80), channel_id=1, source_target_pairs={{1,0},{2,3},{5,4},{6,7},{9,8},{10,11},{13,12},{14,15},{17,16},{18,... | collective-permute-start | bytes 2359304 | tf_op jit(solution)/shard_map/ppermute | solution.py:25
  103.7 29.3 %collective-permute-start.32 = (bf16[1,768,256]{2,1,0:T(8,128)(2,1)S(1)}, bf16[1,768,256]{2,1,0:T(8,128)(2,1)S(1)}, u32[]{:S(2)}, u32[]{:S(2)}) collective-permute-start(bf16[1,768,256]{2,1,0:T(8,128)(2,1)S(1)} %get-tuple-element.76), channel_id=1, source_target_pairs={{1,3},{2,0},{5,7},{6,4},{9,11},{10,8},{13,15},{14,12},{17,19},{18,... | collective-permute-start | bytes 1179656 | tf_op jit(solution)/shard_map/ppermute | solution.py:25
  105.8 46.8 %collective-permute-start.36 = (bf16[1,1280,256]{2,1,0:T(8,128)(2,1)S(1)}, bf16[1,1280,256]{2,1,0:T(8,128)(2,1)S(1)}, u32[]{:S(2)}, u32[]{:S(2)}) collective-permute-start(bf16[1,1280,256]{2,1,0:T(8,128)(2,1)S(1)} %get-tuple-element.84), channel_id=1, source_target_pairs={{1,3},{2,0},{5,7},{6,4},{9,11},{10,8},{13,15},{14,12},{17,19},{18,... | collective-permute-start | bytes 1966088 | tf_op jit(solution)/shard_map/ppermute | solution.py:25
  116.8 32.6 %collective-permute-start.37 = (bf16[1,512,256]{2,1,0:T(8,128)(2,1)}, bf16[1,512,256]{2,1,0:T(8,128)(2,1)S(1)}, u32[]{:S(2)}, u32[]{:S(2)}) collective-permute-start(bf16[1,512,256]{2,1,0:T(8,128)(2,1)} %copy-done.8), channel_id=1, source_target_pairs={{0,2},{3,1},{4,6},{7,5},{8,10},{11,9},{12,14},{15,13},{16,18},{19,... | collective-permute-start | bytes 786440 | tf_op jit(solution)/shard_map/ppermute | solution.py:25
  133.0 19.6 %collective-permute-start.38 = (bf16[1,512,256]{2,1,0:T(8,128)(2,1)S(1)}, bf16[1,512,256]{2,1,0:T(8,128)(2,1)S(1)}, u32[]{:S(2)}, u32[]{:S(2)}) collective-permute-start(bf16[1,512,256]{2,1,0:T(8,128)(2,1)S(1)} %get-tuple-element.88), channel_id=1, source_target_pairs={{1,0},{2,3},{5,4},{6,7},{9,8},{10,11},{13,12},{14,15},{17,16},{18,... | collective-permute-start | bytes 786440 | tf_op jit(solution)/shard_map/ppermute | solution.py:25
  (38 other events, 244.0 us)

commit v3 on v2

--- a/solution.py
+++ b/solution.py
@@ -130,22 +130,34 @@
     return call(divide_kernel, 4, [VMEM], outs, [], x)
 
 
-def own_gram_kernel(*refs):
-    blocks, (mine, sent, acc) = refs[:-3], refs[-3:]
-    total = None
-    for block in blocks:
-        for h in range(block.shape[0]):
-            x = block[h]
-            part = dot_t(x, x)
-            total = part if total is None else total + part
-    acc[...] = total
-    write_halves(acc, mine, sent)
-
-
-def own_gram(blocks):
-    width = blocks[0].shape[-1]
-    scratch = [pltpu.VMEM((width, width), F32)]
-    return call(own_gram_kernel, 12, [VMEM] * len(blocks), halves(width), scratch, *blocks)
+def own_gram_kernel(x_ref, mine, sent, acc):
+    step = pl.program_id(0)
+
+    @pl.when(step == 0)
+    def _():
+        acc[...] = jnp.zeros_like(acc)
+
+    x = x_ref[...]
+    acc[...] += dot_t(x, x)
+
+    @pl.when(step == pl.num_programs(0) - 1)
+    def _():
+        write_halves(acc, mine, sent)
+
+
+def own_gram(panel):
+    rows, width = panel.shape
+    tile = rows // 4
+    return pl.pallas_call(
+        own_gram_kernel,
+        grid=(rows // tile,),
+        in_specs=[pl.BlockSpec((tile, width), lambda i: (i, 0))],
+        out_specs=[pl.BlockSpec((width // 2, width), lambda i: (0, 0))] * 2,
+        out_shape=halves(width),
+        scratch_shapes=[pltpu.VMEM((width, width), F32)],
+        compiler_params=pltpu.CompilerParams(vmem_limit_bytes=48 * 2**20),
+        name="own_gram",
+    )(panel)
 
 
 def cross_kernel(begin, level, chained, last, own, other, *refs):
@@ -476,9 +488,11 @@
     pass_on = send(across, middle)
     cuts = [(0, 1, 0, cut), (0, 1, cut, tail), (0, 0, 0, block_rows), (1, 0, 0, cut),
             (1, 0, cut, tail)]
-    near_own, tail_own, mine, leave_head, leave_tail = pick(after(snapshot_basis, far_own), 48, cuts)
-
-    own_halves = own_gram([far_own, across, near_own, tail_own, mine])
+    near_own, tail_own, mine, leave_head, leave_tail = pick(
+        after(snapshot_basis, far_own), 48, cuts
+    )
+
+    own_halves = own_gram(snapshot_basis)
     own_sum = scatter_space(*own_halves)
     turned = [own_sum] + [swap(own_sum, "group", k) for k in (1, 2, 3)]
 

time: 186 us -> 185 us (level)
  waiting for transfers between devices: 82.3 us -> 79.7 us
  local copies, waits for them, and re-layouts: 3.43 us -> 5.63 us
    pallas_call x18 -> x17, Pallas kernels: 27.6 us -> 24.7 us  [call(): pl.pallas_call(kernel, in_specs=in_specs, out_specs=[VMEM] * len(outs), o...]
    ppermute x42, waiting for transfers between devices: 33.1 us -> 30.4 us  [swap(): return lax.ppermute(block, axis, [(i, i ^ offset) for i in range(count)])]
    unnamed x18 -> x20, local copies, waits for them, and re-layouts: 3.41 us -> 5.61 us
    pallas_call x0 -> x1, Pallas kernels: none -> 2.02 us  [own_gram(): pl.pallas_call(own_gram_kernel, grid=(rows // tile,), in_specs=[pl.BlockS...]
  transfers between devices with their start and end apart: 53 -> 53, of which waited for: 28 -> 26; matrix products, arithmetic and copies ran while one was open for 1% -> 1% of each run, Pallas kernels for 10% -> 13%
where the time goes in v3:
time: 185 us; the launch traced here: 184 us
  waiting for transfers between devices  79.7 us (43%)
  starting transfers between devices  62 us (34%)
  Pallas kernels  34.6 us (19%)
  local copies, waits for them, and re-layouts  5.63 us (3%)
    ppermute x11, waiting for transfers between devices, send(): return lax.ppermute(value, 'group', routes)  49.3 us
    ppermute x42, starting transfers between devices, swap(): return lax.ppermute(block, axis, [(i, i ^ offset) for i in range(count)])  39.3 us
    ppermute x42, waiting for transfers between devices, swap(): return lax.ppermute(block, axis, [(i, i ^ offset) for i in range(count)])  30.4 us
    pallas_call x17, Pallas kernels, call(): pl.pallas_call(kernel, in_specs=in_specs, out_specs=[VMEM] * len(outs), o...  24.7 us
    ppermute x11, starting transfers between devices, send(): return lax.ppermute(value, 'group', routes)  22.7 us
    pallas_call x1, Pallas kernels, merge_filter(): pl.pallas_call(functools.partial(merge_filter_kernel, level, last, len(ot...  7.85 us
    unnamed x20, local copies, waits for them, and re-layouts  5.61 us
  transfers between devices with their start and end apart: 53, of which 26 were waited for; matrix products, arithmetic and copies ran while one was open for 1% of the time, Pallas kernels for 13%

profile of v3, /device:TPU:0, one launch (start us, length us, event | category | flops | bytes accessed | tf_op | source)
XLA Modules:
  0.0 184.0 jit_solution(17627983465119389731)
XLA Ops:
  0.0 2.2 %copy-done = bf16[8192,256]{1,0:T(8,128)(2,1)S(1)} copy-done((bf16[8192,256]{1,0:T(8,128)(2,1)S(1)}, bf16[8192,256]{1,0:T(8,128)(2,1)}, u32[]{:S(2)}) %copy-start) | copy-done | bytes 4194328
  2.2 2.0 %own_gram.1 = (f32[128,256]{1,0:T(8,128)S(1)}, f32[128,256]{1,0:T(8,128)S(1)}) custom-call(bf16[8192,256]{1,0:T(8,128)(2,1)S(1)} %copy-done), custom_call_target="tpu_custom_call" | custom-call | tf_op jit(solution)/shard_map/own_gram/pallas_call | solution.py:151
  5.8 2.9 %collective-permute-start.1 = (f32[32,256]{1,0:T(8,128)S(1)}, f32[32,256]{1,0:T(8,128)S(1)}, u32[]{:S(2)}, u32[]{:S(2)}) collective-permute-start(f32[32,256]{1,0:T(8,128)S(1)} %get-tuple-element.54), channel_id=1, source_target_pairs={{0,8},{4,12},{8,0},{12,4},{16,24},{20,28},{24,16},{28,20},{1,9},{5... | collective-permute-start | bytes 98312 | tf_op jit(solution)/shard_map/ppermute | solution.py:21
  10.2 2.9 %shard_map.30 = (bf16[1,2048,256]{2,1,0:T(8,128)(2,1)}, bf16[1,2048,256]{2,1,0:T(8,128)(2,1)}) custom-call(bf16[8192,256]{1,0:T(8,128)(2,1)} %x_ref.4), custom_call_target="tpu_custom_call" | custom-call | tf_op jit(solution)/shard_map/pallas_call | solution.py:56
  13.1 2.1 %collective-permute-start.16 = (bf16[1,2048,256]{2,1,0:T(8,128)(2,1)}, bf16[1,2048,256]{2,1,0:T(8,128)(2,1)S(1)}, u32[]{:S(2)}, u32[]{:S(2)}) collective-permute-start(bf16[1,2048,256]{2,1,0:T(8,128)(2,1)} %get-tuple-element.73), channel_id=1, source_target_pairs={{0,1},{1,0},{2,3},{3,2},{4,5},{5,4},{6,7},{7,6},{8,9},{9,8},{10,11... | collective-permute-start | bytes 3145736 | tf_op jit(solution)/shard_map/ppermute | solution.py:25
  20.5 3.9 %collective-permute-start.14 = (bf16[1,512,256]{2,1,0:T(8,128)(2,1)S(1)}, bf16[1,512,256]{2,1,0:T(8,128)(2,1)S(1)}, u32[]{:S(2)}, u32[]{:S(2)}) collective-permute-start(bf16[1,512,256]{2,1,0:T(8,128)(2,1)S(1)} %get-tuple-element.61), channel_id=1, source_target_pairs={{0,1},{1,0},{2,3},{3,2},{4,5},{5,4},{6,7},{7,6},{8,9},{9,8},{10,11... | collective-permute-start | bytes 786440 | tf_op jit(solution)/shard_map/ppermute | solution.py:25
  25.7 34.8 %collective-permute-done.14.other.near_tail = bf16[1,512,256]{2,1,0:T(8,128)(2,1)S(1)} collective-permute-done((bf16[1,512,256]{2,1,0:T(8,128)(2,1)S(1)}, bf16[1,512,256]{2,1,0:T(8,128)(2,1)S(1)}, u32[]{:S(2)}, u32[]{:S(2)}) %collective-permute-start.14) | collective-permute-done | bytes 262176 | tf_op jit(solution)/shard_map/ppermute | solution.py:25
  60.5 3.1 %collective-permute-start.5 = (f32[32,256]{1,0:T(8,128)S(1)}, f32[32,256]{1,0:T(8,128)S(1)}, u32[]{:S(2)}, u32[]{:S(2)}) collective-permute-start(f32[32,256]{1,0:T(8,128)S(1)} %add_add_fusion.2), channel_id=1, source_target_pairs={{0,2},{1,3},{2,0},{3,1},{4,6},{5,7},{6,4},{7,5},{8,10},{9,11},{10,... | collective-permute-start | bytes 98312 | tf_op jit(solution)/shard_map/ppermute | solution.py:21
  63.6 1.9 %collective-permute-start.4 = (f32[32,256]{1,0:T(8,128)S(1)}, f32[32,256]{1,0:T(8,128)S(1)}, u32[]{:S(2)}, u32[]{:S(2)}) collective-permute-start(f32[32,256]{1,0:T(8,128)S(1)} %add_add_fusion.2), channel_id=1, source_target_pairs={{0,1},{1,0},{2,3},{3,2},{4,5},{5,4},{6,7},{7,6},{8,9},{9,8},{10,11... | collective-permute-start | bytes 98312 | tf_op jit(solution)/shard_map/ppermute | solution.py:21
  75.2 2.5 %collective-permute-start.12 = (f32[4,32,256]{2,1,0:T(8,128)S(1)}, f32[4,32,256]{2,1,0:T(8,128)S(1)}, u32[]{:S(2)}, u32[]{:S(2)}) collective-permute-start(f32[4,32,256]{2,1,0:T(8,128)S(1)} %pad_maximum_fusion.1.refs_0_), channel_id=1, source_target_pairs={{0,24},{4,28},{8,16},{12,20},{16,8},{20,12},{24,0},{28,4},{1,25},{... | collective-permute-start | bytes 393224 | tf_op jit(solution)/shard_map/ppermute | solution.py:21
  83.7 2.2 %collective-permute-start.22 = (f32[32,256]{1,0:T(8,128)}, f32[32,256]{1,0:T(8,128)}, u32[]{:S(2)}, u32[]{:S(2)}) collective-permute-start(f32[32,256]{1,0:T(8,128)} %add_add_fusion.1), channel_id=1, source_target_pairs={{0,2},{1,3},{2,0},{3,1},{4,6},{5,7},{6,4},{7,5},{8,10},{9,11},{10,... | collective-permute-start | bytes 98312 | tf_op jit(solution)/shard_map/ppermute | solution.py:21
  88.4 4.4 %collective-permute-done.22 = f32[32,256]{1,0:T(8,128)} collective-permute-done((f32[32,256]{1,0:T(8,128)}, f32[32,256]{1,0:T(8,128)}, u32[]{:S(2)}, u32[]{:S(2)}) %collective-permute-start.22) | collective-permute-done | bytes 32800 | tf_op jit(solution)/shard_map/ppermute | solution.py:21
  94.1 3.0 %collective-permute-start.33 = (bf16[1,1536,256]{2,1,0:T(8,128)(2,1)}, bf16[1,1536,256]{2,1,0:T(8,128)(2,1)S(1)}, u32[]{:S(2)}, u32[]{:S(2)}) collective-permute-start(bf16[1,1536,256]{2,1,0:T(8,128)(2,1)} %copy-done.8), channel_id=1, source_target_pairs={{0,2},{3,1},{4,6},{7,5},{8,10},{11,9},{12,14},{15,13},{16,18},{19,... | collective-permute-start | bytes 2359304 | tf_op jit(solution)/shard_map/ppermute | solution.py:25
  98.5 2.5 %collective-permute-start.29 = (f32[2,32,256]{2,1,0:T(8,128)S(1)}, f32[2,32,256]{2,1,0:T(8,128)S(1)}, u32[]{:S(2)}, u32[]{:S(2)}) collective-permute-start(f32[2,32,256]{2,1,0:T(8,128)S(1)} %pad_maximum_fusion.2.refs_0_), channel_id=1, source_target_pairs={{0,24},{4,28},{8,16},{12,20},{16,8},{20,12},{24,0},{28,4},{1,25},{... | collective-permute-start | bytes 196616 | tf_op jit(solution)/shard_map/ppermute | solution.py:21
  106.6 3.1 %collective-permute-done.25.refs_2_ = f32[2,32,256]{2,1,0:T(8,128)S(1)} collective-permute-done((f32[2,32,256]{2,1,0:T(8,128)S(1)}, f32[2,32,256]{2,1,0:T(8,128)S(1)}, u32[]{:S(2)}, u32[]{:S(2)}) %collective-permute-start.25) | collective-permute-done | bytes 65568 | tf_op jit(solution)/shard_map/ppermute | solution.py:21
  114.7 5.1 %collective-permute-start.37 = (bf16[1,512,256]{2,1,0:T(8,128)(2,1)}, bf16[1,512,256]{2,1,0:T(8,128)(2,1)S(1)}, u32[]{:S(2)}, u32[]{:S(2)}) collective-permute-start(bf16[1,512,256]{2,1,0:T(8,128)(2,1)} %copy-done.9), channel_id=1, source_target_pairs={{0,2},{3,1},{4,6},{7,5},{8,10},{11,9},{12,14},{15,13},{16,18},{19,... | collective-permute-start | bytes 786440 | tf_op jit(solution)/shard_map/ppermute | solution.py:25
  119.9 11.1 %collective-permute-done.32.risen = bf16[1,768,256]{2,1,0:T(8,128)(2,1)S(1)} collective-permute-done((bf16[1,768,256]{2,1,0:T(8,128)(2,1)S(1)}, bf16[1,768,256]{2,1,0:T(8,128)(2,1)S(1)}, u32[]{:S(2)}, u32[]{:S(2)}) %collective-permute-start.32) | collective-permute-done | bytes 393248 | tf_op jit(solution)/shard_map/ppermute | solution.py:25
  136.3 9.2 %shard_map.36 = (bf16[2,2,256,256]{3,2,1,0:T(8,128)(2,1)S(1)}, f32[2,512,512]{2,1,0:T(8,128)S(1)}) custom-call(f32[4,256,256]{2,1,0:T(8,128)S(1)} %shard_map.29.diag, f32[2,512,256]{2,1,0:T(8,128)S(1)} %copy-done.1, f32[2,32,256]{2,1,0:T(8,128)S(1)} %pad_maximum_fusion.2.refs_0_, f32[2,32,256]{2,1,0:T(8,128)S(1)} %collective-permute-done.24.refs_1_, ...), custom_call_target="tpu_custom_call" | custom-call | tf_op jit(solution)/shard_map/pallas_call | solution.py:56
  147.1 3.4 %collective-permute-done.38.refs_3_ = bf16[1,512,256]{2,1,0:T(8,128)(2,1)S(1)} collective-permute-done((bf16[1,512,256]{2,1,0:T(8,128)(2,1)S(1)}, bf16[1,512,256]{2,1,0:T(8,128)(2,1)S(1)}, u32[]{:S(2)}, u32[]{:S(2)}) %collective-permute-start.38) | collective-permute-done | bytes 262176 | tf_op jit(solution)/shard_map/ppermute | solution.py:25
  158.5 2.4 %collective-permute-done.42 = f32[32,256]{1,0:T(8,128)S(1)} collective-permute-done((f32[32,256]{1,0:T(8,128)S(1)}, f32[32,256]{1,0:T(8,128)S(1)}, u32[]{:S(2)}, u32[]{:S(2)}) %collective-permute-start.42) | collective-permute-done | bytes 32800 | tf_op jit(solution)/shard_map/ppermute | solution.py:21
  161.0 2.3 %collective-permute-start.45 = (f32[32,256]{1,0:T(8,128)S(1)}, f32[32,256]{1,0:T(8,128)S(1)}, u32[]{:S(2)}, u32[]{:S(2)}) collective-permute-start(f32[32,256]{1,0:T(8,128)S(1)} %add_add_fusion), channel_id=1, source_target_pairs={{0,3},{1,2},{2,1},{3,0},{4,7},{5,6},{6,5},{7,4},{8,11},{9,10},{10,... | collective-permute-start | bytes 98312 | tf_op jit(solution)/shard_map/ppermute | solution.py:21
  163.3 2.2 %collective-permute-start.43 = (f32[32,256]{1,0:T(8,128)S(1)}, f32[32,256]{1,0:T(8,128)S(1)}, u32[]{:S(2)}, u32[]{:S(2)}) collective-permute-start(f32[32,256]{1,0:T(8,128)S(1)} %add_add_fusion), channel_id=1, source_target_pairs={{0,1},{1,0},{2,3},{3,2},{4,5},{5,4},{6,7},{7,6},{8,9},{9,8},{10,11... | collective-permute-start | bytes 98312 | tf_op jit(solution)/shard_map/ppermute | solution.py:21
  174.1 1.9 %shard_map.37.diag = f32[2,256,256]{2,1,0:T(8,128)S(1)} custom-call(f32[2,512,512]{2,1,0:T(8,128)S(1)} %get-tuple-element.71.gram, bf16[2,2,256,256]{3,2,1,0:T(8,128)(2,1)S(1)} %get-tuple-element.72.mix), custom_call_target="tpu_custom_call" | custom-call | tf_op jit(solution)/shard_map/pallas_call | solution.py:56
  176.0 7.8 %merge_filter.1 = bf16[1,2048,256]{2,1,0:T(8,128)(2,1)} custom-call(f32[2,256,256]{2,1,0:T(8,128)S(1)} %shard_map.37.diag, f32[2,512,256]{2,1,0:T(8,128)S(1)} %copy-done.1, bf16[1,2048,256]{2,1,0:T(8,128)(2,1)S(1)} %shard_map.38.own, bf16[1,768,256]{2,1,0:T(8,128)(2,1)S(1)} %get-tuple-element.81.refs_0_, ...), custom_call_target="tpu_custom_call" | custom-call | tf_op jit(solution)/shard_map/merge_filter/pallas_call | solution.py:456
  (130 shorter events, 64.4 us)
Async XLA Ops:
  5.8 12.9 %collective-permute-start.1 = (f32[32,256]{1,0:T(8,128)S(1)}, f32[32,256]{1,0:T(8,128)S(1)}, u32[]{:S(2)}, u32[]{:S(2)}) collective-permute-start(f32[32,256]{1,0:T(8,128)S(1)} %get-tuple-element.54), channel_id=1, source_target_pairs={{0,8},{4,12},{8,0},{12,4},{16,24},{20,28},{24,16},{28,20},{1,9},{5... | collective-permute-start | bytes 98312 | tf_op jit(solution)/shard_map/ppermute | solution.py:21
  8.7 10.0 %collective-permute-start.2 = (f32[32,256]{1,0:T(8,128)S(1)}, f32[32,256]{1,0:T(8,128)S(1)}, u32[]{:S(2)}, u32[]{:S(2)}) collective-permute-start(f32[32,256]{1,0:T(8,128)S(1)} %get-tuple-element.55), channel_id=1, source_target_pairs={{0,16},{4,20},{8,24},{12,28},{16,0},{20,4},{24,8},{28,12},{1,17},{... | collective-permute-start | bytes 98312 | tf_op jit(solution)/shard_map/ppermute | solution.py:21
  10.2 8.5 %collective-permute-start.3 = (f32[32,256]{1,0:T(8,128)S(1)}, f32[32,256]{1,0:T(8,128)S(1)}, u32[]{:S(2)}, u32[]{:S(2)}) collective-permute-start(f32[32,256]{1,0:T(8,128)S(1)} %get-tuple-element.56), channel_id=1, source_target_pairs={{0,24},{4,28},{8,16},{12,20},{16,8},{20,12},{24,0},{28,4},{1,25},{... | collective-permute-start | bytes 98312 | tf_op jit(solution)/shard_map/ppermute | solution.py:21
  13.1 52.5 %collective-permute-start.16 = (bf16[1,2048,256]{2,1,0:T(8,128)(2,1)}, bf16[1,2048,256]{2,1,0:T(8,128)(2,1)S(1)}, u32[]{:S(2)}, u32[]{:S(2)}) collective-permute-start(bf16[1,2048,256]{2,1,0:T(8,128)(2,1)} %get-tuple-element.73), channel_id=1, source_target_pairs={{0,1},{1,0},{2,3},{3,2},{4,5},{5,4},{6,7},{7,6},{8,9},{9,8},{10,11... | collective-permute-start | bytes 3145736 | tf_op jit(solution)/shard_map/ppermute | solution.py:25
  18.7 44.9 %collective-permute-start.15 = (bf16[1,1536,256]{2,1,0:T(8,128)(2,1)S(1)}, bf16[1,1536,256]{2,1,0:T(8,128)(2,1)S(1)}, u32[]{:S(2)}, u32[]{:S(2)}) collective-permute-start(bf16[1,1536,256]{2,1,0:T(8,128)(2,1)S(1)} %get-tuple-element.63), channel_id=1, source_target_pairs={{0,1},{1,0},{2,3},{3,2},{4,5},{5,4},{6,7},{7,6},{8,9},{9,8},{10,11... | collective-permute-start | bytes 2359304 | tf_op jit(solution)/shard_map/ppermute | solution.py:25
  18.8 67.1 %collective-permute-start.34 = (bf16[1,2048,256]{2,1,0:T(8,128)(2,1)}, bf16[1,2048,256]{2,1,0:T(8,128)(2,1)}, u32[]{:S(2)}, u32[]{:S(2)}) collective-permute-start(bf16[1,2048,256]{2,1,0:T(8,128)(2,1)} %get-tuple-element.64.own), channel_id=1, source_target_pairs={{1,2},{2,1},{5,6},{6,5},{9,10},{10,9},{13,14},{14,13},{17,18},{18,... | collective-permute-start | bytes 3145736 | tf_op jit(solution)/shard_map/ppermute | solution.py:25
  20.5 40.1 %collective-permute-start.14 = (bf16[1,512,256]{2,1,0:T(8,128)(2,1)S(1)}, bf16[1,512,256]{2,1,0:T(8,128)(2,1)S(1)}, u32[]{:S(2)}, u32[]{:S(2)}) collective-permute-start(bf16[1,512,256]{2,1,0:T(8,128)(2,1)S(1)} %get-tuple-element.61), channel_id=1, source_target_pairs={{0,1},{1,0},{2,3},{3,2},{4,5},{5,4},{6,7},{7,6},{8,9},{9,8},{10,11... | collective-permute-start | bytes 786440 | tf_op jit(solution)/shard_map/ppermute | solution.py:25
  24.4 45.4 %collective-permute-start.6 = (f32[32,256]{1,0:T(8,128)S(1)}, f32[32,256]{1,0:T(8,128)S(1)}, u32[]{:S(2)}, u32[]{:S(2)}) collective-permute-start(f32[32,256]{1,0:T(8,128)S(1)} %add_add_fusion.2), channel_id=1, source_target_pairs={{0,3},{1,2},{2,1},{3,0},{4,7},{5,6},{6,5},{7,4},{8,11},{9,10},{10,... | collective-permute-start | bytes 98312 | tf_op jit(solution)/shard_map/ppermute | solution.py:21
  60.5 9.3 %collective-permute-start.5 = (f32[32,256]{1,0:T(8,128)S(1)}, f32[32,256]{1,0:T(8,128)S(1)}, u32[]{:S(2)}, u32[]{:S(2)}) collective-permute-start(f32[32,256]{1,0:T(8,128)S(1)} %add_add_fusion.2), channel_id=1, source_target_pairs={{0,2},{1,3},{2,0},{3,1},{4,6},{5,7},{6,4},{7,5},{8,10},{9,11},{10,... | collective-permute-start | bytes 98312 | tf_op jit(solution)/shard_map/ppermute | solution.py:21
  63.6 6.2 %collective-permute-start.4 = (f32[32,256]{1,0:T(8,128)S(1)}, f32[32,256]{1,0:T(8,128)S(1)}, u32[]{:S(2)}, u32[]{:S(2)}) collective-permute-start(f32[32,256]{1,0:T(8,128)S(1)} %add_add_fusion.2), channel_id=1, source_target_pairs={{0,1},{1,0},{2,3},{3,2},{4,5},{5,4},{6,7},{7,6},{8,9},{9,8},{10,11... | collective-permute-start | bytes 98312 | tf_op jit(solution)/shard_map/ppermute | solution.py:21
  65.6 36.1 %collective-permute-start.31 = (bf16[1,2048,256]{2,1,0:T(8,128)(2,1)}, bf16[1,2048,256]{2,1,0:T(8,128)(2,1)}, u32[]{:S(2)}, u32[]{:S(2)}) collective-permute-start(bf16[1,2048,256]{2,1,0:T(8,128)(2,1)} %get-tuple-element.73), channel_id=1, source_target_pairs={{1,2},{2,1},{5,6},{6,5},{9,10},{10,9},{13,14},{14,13},{17,18},{18,... | collective-permute-start | bytes 3145736 | tf_op jit(solution)/shard_map/ppermute | solution.py:25
  75.2 6.7 %collective-permute-start.12 = (f32[4,32,256]{2,1,0:T(8,128)S(1)}, f32[4,32,256]{2,1,0:T(8,128)S(1)}, u32[]{:S(2)}, u32[]{:S(2)}) collective-permute-start(f32[4,32,256]{2,1,0:T(8,128)S(1)} %pad_maximum_fusion.1.refs_0_), channel_id=1, source_target_pairs={{0,24},{4,28},{8,16},{12,20},{16,8},{20,12},{24,0},{28,4},{1,25},{... | collective-permute-start | bytes 393224 | tf_op jit(solution)/shard_map/ppermute | solution.py:21
  79.5 8.3 %collective-permute-start.8 = (f32[4,32,256]{2,1,0:T(8,128)S(1)}, f32[4,32,256]{2,1,0:T(8,128)}, u32[]{:S(2)}, u32[]{:S(2)}) collective-permute-start(f32[4,32,256]{2,1,0:T(8,128)S(1)} %pad_maximum_fusion.1.refs_0_), channel_id=1, source_target_pairs={{0,8},{4,12},{8,0},{12,4},{16,24},{20,28},{24,16},{28,20},{1,9},{5... | collective-permute-start | bytes 393224 | tf_op jit(solution)/shard_map/ppermute | solution.py:21
  83.7 9.1 %collective-permute-start.22 = (f32[32,256]{1,0:T(8,128)}, f32[32,256]{1,0:T(8,128)}, u32[]{:S(2)}, u32[]{:S(2)}) collective-permute-start(f32[32,256]{1,0:T(8,128)} %add_add_fusion.1), channel_id=1, source_target_pairs={{0,2},{1,3},{2,0},{3,1},{4,6},{5,7},{6,4},{7,5},{8,10},{9,11},{10,... | collective-permute-start | bytes 98312 | tf_op jit(solution)/shard_map/ppermute | solution.py:21
  85.9 6.9 %collective-permute-start.21 = (f32[32,256]{1,0:T(8,128)}, f32[32,256]{1,0:T(8,128)}, u32[]{:S(2)}, u32[]{:S(2)}) collective-permute-start(f32[32,256]{1,0:T(8,128)} %add_add_fusion.1), channel_id=1, source_target_pairs={{0,1},{1,0},{2,3},{3,2},{4,5},{5,4},{6,7},{7,6},{8,9},{9,8},{10,11... | collective-permute-start | bytes 98312 | tf_op jit(solution)/shard_map/ppermute | solution.py:21
  87.8 6.3 %collective-permute-start.7 = (f32[4,32,256]{2,1,0:T(8,128)S(1)}, f32[4,32,256]{2,1,0:T(8,128)S(1)}, u32[]{:S(2)}, u32[]{:S(2)}) collective-permute-start(f32[4,32,256]{2,1,0:T(8,128)S(1)} %pad_maximum_fusion.1.refs_0_), channel_id=1, source_target_pairs={{0,4},{4,0},{8,12},{12,8},{16,20},{20,16},{24,28},{28,24},{1,5},{5... | collective-permute-start | bytes 393224 | tf_op jit(solution)/shard_map/ppermute | solution.py:21
  88.1 9.1 %collective-permute-start.13 = (f32[4,32,256]{2,1,0:T(8,128)}, f32[4,32,256]{2,1,0:T(8,128)S(1)}, u32[]{:S(2)}, u32[]{:S(2)}) collective-permute-start(f32[4,32,256]{2,1,0:T(8,128)} %copy-done.4), channel_id=1, source_target_pairs={{0,4},{4,0},{8,12},{12,8},{16,20},{20,16},{24,28},{28,24},{1,5},{5... | collective-permute-start | bytes 393224 | tf_op jit(solution)/shard_map/ppermute | solution.py:21
  92.8 8.3 %collective-permute-start.9 = (f32[4,32,256]{2,1,0:T(8,128)}, f32[4,32,256]{2,1,0:T(8,128)S(1)}, u32[]{:S(2)}, u32[]{:S(2)}) collective-permute-start(f32[4,32,256]{2,1,0:T(8,128)} %collective-permute-done.8.refs_2_), channel_id=1, source_target_pairs={{0,4},{4,0},{8,12},{12,8},{16,20},{20,16},{24,28},{28,24},{1,5},{5... | collective-permute-start | bytes 393224 | tf_op jit(solution)/shard_map/ppermute | solution.py:21
  94.1 52.2 %collective-permute-start.33 = (bf16[1,1536,256]{2,1,0:T(8,128)(2,1)}, bf16[1,1536,256]{2,1,0:T(8,128)(2,1)S(1)}, u32[]{:S(2)}, u32[]{:S(2)}) collective-permute-start(bf16[1,1536,256]{2,1,0:T(8,128)(2,1)} %copy-done.8), channel_id=1, source_target_pairs={{0,2},{3,1},{4,6},{7,5},{8,10},{11,9},{12,14},{15,13},{16,18},{19,... | collective-permute-start | bytes 2359304 | tf_op jit(solution)/shard_map/ppermute | solution.py:25
  97.1 49.2 %collective-permute-start.35 = (bf16[1,1536,256]{2,1,0:T(8,128)(2,1)S(1)}, bf16[1,1536,256]{2,1,0:T(8,128)(2,1)S(1)}, u32[]{:S(2)}, u32[]{:S(2)}) collective-permute-start(bf16[1,1536,256]{2,1,0:T(8,128)(2,1)S(1)} %get-tuple-element.80), channel_id=1, source_target_pairs={{1,0},{2,3},{5,4},{6,7},{9,8},{10,11},{13,12},{14,15},{17,16},{18,... | collective-permute-start | bytes 2359304 | tf_op jit(solution)/shard_map/ppermute | solution.py:25
  101.6 29.3 %collective-permute-start.32 = (bf16[1,768,256]{2,1,0:T(8,128)(2,1)S(1)}, bf16[1,768,256]{2,1,0:T(8,128)(2,1)S(1)}, u32[]{:S(2)}, u32[]{:S(2)}) collective-permute-start(bf16[1,768,256]{2,1,0:T(8,128)(2,1)S(1)} %get-tuple-element.76), channel_id=1, source_target_pairs={{1,3},{2,0},{5,7},{6,4},{9,11},{10,8},{13,15},{14,12},{17,19},{18,... | collective-permute-start | bytes 1179656 | tf_op jit(solution)/shard_map/ppermute | solution.py:25
  103.7 46.8 %collective-permute-start.36 = (bf16[1,1280,256]{2,1,0:T(8,128)(2,1)S(1)}, bf16[1,1280,256]{2,1,0:T(8,128)(2,1)S(1)}, u32[]{:S(2)}, u32[]{:S(2)}) collective-permute-start(bf16[1,1280,256]{2,1,0:T(8,128)(2,1)S(1)} %get-tuple-element.84), channel_id=1, source_target_pairs={{1,3},{2,0},{5,7},{6,4},{9,11},{10,8},{13,15},{14,12},{17,19},{18,... | collective-permute-start | bytes 1966088 | tf_op jit(solution)/shard_map/ppermute | solution.py:25
  114.7 32.4 %collective-permute-start.37 = (bf16[1,512,256]{2,1,0:T(8,128)(2,1)}, bf16[1,512,256]{2,1,0:T(8,128)(2,1)S(1)}, u32[]{:S(2)}, u32[]{:S(2)}) collective-permute-start(bf16[1,512,256]{2,1,0:T(8,128)(2,1)} %copy-done.9), channel_id=1, source_target_pairs={{0,2},{3,1},{4,6},{7,5},{8,10},{11,9},{12,14},{15,13},{16,18},{19,... | collective-permute-start | bytes 786440 | tf_op jit(solution)/shard_map/ppermute | solution.py:25
  130.9 19.6 %collective-permute-start.38 = (bf16[1,512,256]{2,1,0:T(8,128)(2,1)S(1)}, bf16[1,512,256]{2,1,0:T(8,128)(2,1)S(1)}, u32[]{:S(2)}, u32[]{:S(2)}) collective-permute-start(bf16[1,512,256]{2,1,0:T(8,128)(2,1)S(1)} %get-tuple-element.88), channel_id=1, source_target_pairs={{1,0},{2,3},{5,4},{6,7},{9,8},{10,11},{13,12},{14,15},{17,16},{18,... | collective-permute-start | bytes 786440 | tf_op jit(solution)/shard_map/ppermute | solution.py:25
  (39 other events, 249.6 us)
